TPU v7x, 32 devices: a whole 2x2x4 slice. The times are simulated.
32 devices in a mesh: slab: 2 (over x), inline: 8 (over z, y), xline: 2 (over core).
Axes of the slice: x: 2, y: 2, z: 4, core: 2. Of those that a mesh axis runs over, the one named last changes fastest.
Arguments:
- traces: bfloat16 [256, 48, 128], P(('slab', 'inline'), 'xline'), parts along dimension 0, may hold values from -15 to 15
- directions: int32 [10], replicated, may hold values from 0 to 31
- init_means: float32 [32, 20], replicated, may hold values from 0.3 to 2.5
- init_variances: float32 [32, 20], replicated, may hold values from 0.01 to 0.2
- init_weights: float32 [32], replicated, may hold values from 0.01 to 1
Outputs:
- posterior: bfloat16 [256, 32, 48, 128], P(('slab', 'inline'), None, 'xline'), parts along dimension 0
- final_means: float32 [64, 20], P('slab'), parts along dimension 0
- final_variances: float32 [64, 20], P('slab'), parts along dimension 0
- final_weights: float32 [64], P('slab'), parts along dimension 0
There are 2 independent parts, one for each index of `slab`. A program takes and returns all parts, laid end to end along the dimension named above; an argument that names none is the same for every part. Nothing has to cross between parts.
All inputs are finite; a program needn't handle non-finite values.
Results may differ from a plain program's by a relative error of at most 0.001.
The roundings to bfloat16 on the way count: a program that leaves them out, or rounds other values in their place, can miss the bound.
Values may be sent and summed in bfloat16 or wider, within the bound.
A program may use at most 64 MiB of HBM per device.

v0:
```python
import functools
import math

import jax
import jax.numpy as jnp
from jax import lax
from jax.experimental import pallas as pl
from jax.experimental.pallas import tpu as pltpu
from jax.sharding import PartitionSpec as P

TAPS = 31
HALF = 15
AZIMUTHS = 8
DIPS = 4
LANES = 128

eps_mag = 0.01
wavenumber = math.pi / 4.0
width_scale = HALF / 3.0
norm = math.sqrt(
    sum(math.exp(-n * n / (width_scale * width_scale)) for n in range(-HALF, HALF + 1))
)
MESH = pl.DeviceIdType.MESH
f32 = jnp.float32
bf16 = jnp.bfloat16
VMEM = pltpu.MemorySpace.VMEM
SMEM = pltpu.MemorySpace.SMEM


def round_up(value, step):
    return -(-value // step) * step


def halo_kernel(inlines, xlines, own_ref, out_ref, send_sem, recv_sem):
    row = lax.axis_index("inline")
    col = lax.axis_index("xline")

    def there(side):
        return row > 0 if side < 0 else row < inlines - 1

    barrier = pltpu.get_barrier_semaphore()
    for side in (-1, 1):
        @pl.when(there(side))
        def _(side=side):
            pl.semaphore_signal(
                barrier, inc=1, device_id={"inline": row + side}, device_id_type=MESH
            )
    for shift in range(1, xlines):
        pl.semaphore_signal(
            barrier,
            inc=1,
            device_id={"xline": lax.rem(col + shift, xlines)},
            device_id_type=MESH,
        )
    sides = (row > 0).astype(jnp.int32) + (row < inlines - 1).astype(jnp.int32)
    pl.semaphore_wait(barrier, sides + xlines - 1)

    def along(side):
        return pltpu.make_async_remote_copy(
            src_ref=own_ref,
            dst_ref=out_ref.at[1 - side, col],
            send_sem=send_sem.at[1 - side, 0],
            recv_sem=recv_sem.at[1 - side, 0],
            device_id={"inline": row + side},
            device_id_type=MESH,
        )

    def across(block, shift):
        return pltpu.make_async_remote_copy(
            src_ref=own_ref if block == 1 else out_ref.at[block, col],
            dst_ref=out_ref.at[block, col],
            send_sem=send_sem.at[block, shift],
            recv_sem=recv_sem.at[block, shift],
            device_id={"xline": lax.rem(col + shift, xlines)},
            device_id_type=MESH,
        )

    for side in (-1, 1):
        @pl.when(there(side))
        def _(side=side):
            along(side).start()
    for shift in range(1, xlines):
        across(1, shift).start()
    out_ref[1, col] = own_ref[...]
    for side in (-1, 1):
        @pl.when(jnp.logical_not(there(side)))
        def _(side=side):
            out_ref[1 + side] = jnp.zeros(out_ref.shape[1:], out_ref.dtype)
    for side in (-1, 1):
        @pl.when(there(side))
        def _(side=side):
            along(-side).wait_recv()
            for shift in range(1, xlines):
                across(1 + side, shift).start()
    for shift in range(1, xlines):
        across(1, shift).wait()
    for side in (-1, 1):
        @pl.when(there(side))
        def _(side=side):
            along(side).wait_send()
            for shift in range(1, xlines):
                across(1 + side, shift).wait()


def gather_halo(traces):
    inlines, xlines = lax.axis_size("inline"), lax.axis_size("xline")
    return pl.pallas_call(
        functools.partial(halo_kernel, inlines, xlines),
        out_shape=jax.ShapeDtypeStruct((3, xlines) + traces.shape, traces.dtype),
        in_specs=[pl.BlockSpec(memory_space=VMEM)],
        out_specs=pl.BlockSpec(memory_space=VMEM),
        scratch_shapes=[
            pltpu.SemaphoreType.DMA((3, xlines)),
            pltpu.SemaphoreType.DMA((3, xlines)),
        ],
        compiler_params=pltpu.CompilerParams(
            collective_id=0, has_side_effects=True, vmem_limit_bytes=4 << 20
        ),
        name="halo",
    )(traces)


def filter_kernel(sizes, dir_ref, halo_ref, out_ref, flat, x_mat, cross):
    rows, cols, width, pad, orients = sizes
    deep = 3 * rows
    group = 8
    orient = pl.program_id(0)

    @pl.when(orient == 0)
    def _():
        for block in range(3):
            for i in range(rows):
                for part in range(width // cols):
                    start = ((block * rows + i) * width) + part * cols
                    flat[start : start + cols, :] = halo_ref[block, part, i]
        for y in range(cols):
            for extra in range(pad - 2 * orients):
                out_ref[y, pl.ds(2 * orients + extra, rows, stride=pad), :] = jnp.full(
                    (rows, LANES), 1.0 if extra == 0 else 0.0, f32
                )

    direction = dir_ref[orient]
    azimuth = jnp.full((8, LANES), (direction % AZIMUTHS).astype(f32)) * (math.pi / AZIMUTHS)
    dip_angle = jnp.full((8, LANES), (direction // AZIMUTHS + 1).astype(f32)) * (
        math.pi / (2 * DIPS + 2)
    )
    waves = [
        wavenumber * (jnp.sin(dip_angle) * jnp.cos(azimuth)),
        wavenumber * (jnp.sin(dip_angle) * jnp.sin(azimuth)),
        wavenumber * jnp.cos(dip_angle),
    ]

    def toeplitz(axis, difference):
        offset = (difference - HALF).astype(f32)
        copies = difference.shape[1] // LANES
        wave = waves[axis]
        phase = offset * (wave if copies == 1 else jnp.concatenate([wave] * copies, axis=1))
        envelope = jnp.exp(-offset * offset / (2.0 * width_scale * width_scale)) / norm
        hit = jnp.logical_and(difference >= 0, difference < TAPS)
        real = jnp.where(hit, envelope * jnp.cos(phase), 0.0)
        imag = jnp.where(hit, envelope * jnp.sin(phase), 0.0)
        return real, imag

    def iotas(shape):
        return (
            lax.broadcasted_iota(jnp.int32, shape, 0),
            lax.broadcasted_iota(jnp.int32, shape, 1),
        )

    def roll(value, amount):
        return value if amount == 0 else pltpu.roll(value, amount, 1)

    sub, lane = iotas((8, LANES))
    bases = toeplitz(2, jnp.bitwise_and(sub - lane + HALF, LANES - 1))
    pieces = []
    for s in range(0, LANES, 8):
        near = jnp.abs(sub + s - lane) <= HALF
        pieces.append(
            jnp.concatenate([jnp.where(near, roll(base, s), 0.0) for base in bases], axis=1)
        )
    time_mat = jnp.concatenate(pieces, axis=0).astype(bf16)

    lanes = round_up(group * width + LANES, LANES)
    sub, lane = iotas((group, lanes))
    difference = lane - sub * width - lax.axis_index("xline") * cols + HALF
    bases = toeplitz(1, jnp.where(difference >= lanes - 64, difference - lanes, difference))
    mine = jnp.logical_and(lane >= sub * width, lane < (sub + 1) * width)
    for part in range(2):
        for y in range(0, cols, 2):
            pair = jnp.concatenate(
                [jnp.where(mine, roll(bases[part], y + dy), 0.0) for dy in range(2)], axis=0
            )
            start = (part * cols + y) * group
            x_mat[start : start + 2 * group, :] = pair[:, : group * width].astype(bf16)

    sub, lane = iotas((8, LANES))
    bases = toeplitz(0, jnp.bitwise_and(lane - sub - rows + HALF, LANES - 1))
    real_first, imag_first = [
        jnp.concatenate(
            [jnp.where(lane < deep, roll(base, j), 0.0) for j in range(0, rows, 8)], axis=0
        )
        for base in bases
    ]
    blank = jnp.zeros((rows, LANES), f32)
    real_first, imag_first = [
        jnp.concatenate([part, blank], axis=1) for part in (real_first, imag_first)
    ]
    real_next, imag_next = pltpu.roll(real_first, deep, 1), pltpu.roll(imag_first, deep, 1)
    base = jnp.concatenate([real_first - imag_next, imag_first + real_next], axis=0)
    i_mat = jnp.concatenate([base, pltpu.roll(base, 2 * deep, 1)], axis=0).astype(bf16)
    i_mat = i_mat[:, : 4 * deep]

    for step in range(deep // group):
        span = group * width
        band = jnp.dot(
            flat[step * span : (step + 1) * span, :],
            time_mat,
            preferred_element_type=f32,
        ).astype(bf16)
        mixed = jnp.dot(x_mat[...], band, preferred_element_type=f32)
        for y in range(cols):
            with_cos = mixed[y * group : (y + 1) * group]
            with_sin = mixed[(cols + y) * group : (cols + y + 1) * group]
            cu, cv = with_cos[:, :LANES], with_cos[:, LANES:]
            su, sv = with_sin[:, :LANES], with_sin[:, LANES:]
            for slot, value in enumerate((cu - sv, su + cv, cu + sv, su - cv)):
                start = (slot * cols + y) * deep + step * group
                cross[start : start + group, :] = value

    half = cols // 2
    for q in range(2):
        for y0 in range(0, half, 2):
            columns = []
            for dy in range(2):
                pieces = []
                for g in range(2):
                    for r in range(2):
                        start = ((q * 2 + r) * cols + y0 + dy + g * half) * deep
                        pieces.append(cross[start : start + deep, :])
                columns.append(jnp.concatenate(pieces, axis=0).astype(bf16))
            total = jnp.dot(i_mat, jnp.concatenate(columns, axis=1), preferred_element_type=f32)
            for g in range(2):
                re = total[g * 2 * rows : g * 2 * rows + rows]
                im = total[g * 2 * rows + rows : (g + 1) * 2 * rows]
                size = jnp.sqrt(re * re + im * im + eps_mag)
                for dy in range(2):
                    out_ref[
                        y0 + dy + g * half, pl.ds(2 * orient + q, rows, stride=pad), :
                    ] = size[:, dy * LANES : (dy + 1) * LANES]


def filter_features(halo, directions, pad):
    _, xlines, rows, cols, samples = halo.shape
    orients = directions.shape[0]
    width = xlines * cols
    sizes = (rows, cols, width, pad, orients)
    return pl.pallas_call(
        functools.partial(filter_kernel, sizes),
        out_shape=jax.ShapeDtypeStruct((cols, rows * pad, samples), f32),
        grid=(orients,),
        in_specs=[
            pl.BlockSpec(memory_space=SMEM),
            pl.BlockSpec(memory_space=VMEM),
        ],
        out_specs=pl.BlockSpec(memory_space=VMEM),
        scratch_shapes=[
            pltpu.VMEM((3 * rows * width, samples), bf16),
            pltpu.VMEM((2 * cols * 8, 8 * width), bf16),
            pltpu.VMEM((4 * cols * 3 * rows, samples), f32),
        ],
        compiler_params=pltpu.CompilerParams(vmem_limit_bytes=20 << 20),
        name="filters",
    )(directions, halo)


def split3(value):
    high = value.astype(bf16)
    rest = value - high.astype(f32)
    mid = rest.astype(bf16)
    low = (rest - mid.astype(f32)).astype(bf16)
    return high, mid, low


def column(row):
    return jnp.transpose(jnp.broadcast_to(row, (row.shape[1], row.shape[1])))


def padded(value, fill):
    rows, lanes = value.shape
    wide = jnp.concatenate([value, jnp.full((rows, LANES - lanes), fill, f32)], axis=1)
    full = jnp.concatenate([wide, jnp.full((LANES - rows, LANES), fill, f32)], axis=0)
    return jnp.transpose(full)


def first_params(mean_ref, var_ref, weight_ref):
    comps = mean_ref.shape[1]
    means = padded(mean_ref[...], 0.0)[:comps]
    shift_row = jnp.mean(means, axis=0, keepdims=True)
    weights = jnp.broadcast_to(padded(weight_ref[...], 1.0)[:comps, :1], (comps, LANES))
    return (means - shift_row, padded(var_ref[...], 1.0)[:comps], weights), shift_row


def next_params(folded, params, sizes):
    pad, count, cells = sizes
    means, spreads, _ = params
    comps = means.shape[0]
    total = jnp.concatenate([folded, pltpu.roll(folded, LANES // 2, 1)], axis=0)
    used = lax.broadcasted_iota(jnp.int32, (comps, LANES), 1) < count
    mass = total[:, count : count + 1]
    first = jnp.where(used, total, 0.0)
    second = jnp.where(used, pltpu.roll(total, LANES - pad, 1), 0.0)
    below = mass + 1.0
    new_means = (first + means) / below
    centred = second - 2.0 * new_means * first + new_means * new_means * mass
    new_spreads = jnp.where(used, (centred + spreads) / below, 1.0)
    return new_means, new_spreads, jnp.broadcast_to(below / (cells + comps), (comps, LANES))


def peer(shift, inlines, xlines):
    me = lax.axis_index("inline") * xlines + lax.axis_index("xline")
    other = lax.rem(me + shift, inlines * xlines)
    return {"inline": other // xlines, "xline": lax.rem(other, xlines)}


def greet(inlines, xlines):
    barrier = pltpu.get_barrier_semaphore()
    for shift in range(1, inlines * xlines):
        pl.semaphore_signal(
            barrier, inc=1, device_id=peer(shift, inlines, xlines), device_id_type=MESH
        )


def gather_sum(inlines, xlines, payload_ref, slots, send_sem, recv_sem):
    members = inlines * xlines
    me = lax.axis_index("inline") * xlines + lax.axis_index("xline")
    pl.semaphore_wait(pltpu.get_barrier_semaphore(), members - 1)

    def copy(shift):
        return pltpu.make_async_remote_copy(
            src_ref=payload_ref,
            dst_ref=slots.at[me],
            send_sem=send_sem.at[shift],
            recv_sem=recv_sem.at[shift],
            device_id=peer(shift, inlines, xlines),
            device_id_type=MESH,
        )

    for shift in range(1, members):
        copy(shift).start()
    slots[me] = payload_ref[...]
    for shift in range(1, members):
        copy(shift).wait()
    total = slots[0]
    for member in range(1, members):
        total = total + slots[member]
    return total


def gather_scratch(members, comps):
    return [
        pltpu.VMEM((members, comps // 2, LANES), f32),
        pltpu.SemaphoreType.DMA((members,)),
        pltpu.SemaphoreType.DMA((members,)),
    ]


def moment_kernel(sizes, last, *refs):
    cols, pad, count, chunk, together, cells, inlines, xlines = sizes
    if last:
        split_ref, sum_ref, mean_ref, var_ref, weight_ref, *refs = refs
        moment_ref, post_ref, table, total, wide = refs
    else:
        feat_ref, mean_ref, var_ref, weight_ref, *refs = refs
        moment_ref, split_ref, table, total, shift_ref, payload, slots, send_sem, recv_sem = refs
    step = pl.program_id(0)
    comps = mean_ref.shape[1]

    @pl.when(step == 0)
    def _():
        if not last:
            greet(inlines, xlines)
        params, shift_row = first_params(mean_ref, var_ref, weight_ref)
        if last:
            params = next_params(sum_ref[...], params, (pad, count, cells))
        else:
            shift_ref[...] = column(shift_row)[:pad]
        lane = lax.broadcasted_iota(jnp.int32, (comps, 2 * LANES), 1)
        means = jnp.concatenate([params[0], jnp.zeros((comps, LANES), f32)], axis=1)
        spreads = jnp.concatenate([params[1], jnp.ones((comps, LANES), f32)], axis=1)
        used = lane < count
        inverse = jnp.where(used, 1.0 / spreads, 0.0)
        scaled = means * inverse
        terms = jnp.where(used, jnp.log(2.0 * math.pi * spreads) + means * scaled, 0.0)
        constant = jnp.log(params[2][:, :1]) - 0.5 * jnp.sum(terms, axis=1, keepdims=True)
        row = jnp.where(used, scaled, 0.0) + jnp.where(lane == count, constant, 0.0)
        row = row + pltpu.roll(-0.5 * inverse, pad, 1)
        parts = split3(row)
        for index, part in enumerate(parts):
            part = part.astype(f32)
            tiled = part + pltpu.roll(part, 2 * pad, 1) + pltpu.roll(part, 4 * pad, 1)
            table[index * comps : (index + 1) * comps, :] = tiled.astype(bf16)
        total[...] = jnp.zeros_like(total)

    weights = table[:, : 6 * pad]
    def scores(j, first):
        span = slice(first * LANES, (first + chunk) * LANES)
        if last:
            operand = split_ref[j, :, span]
        else:
            base = pl.multiple_of((step * together + j) * pad, 8)
            values = jnp.concatenate(
                [
                    feat_ref[first + y, pl.ds(base, pad), :] - shift_ref[...]
                    for y in range(chunk)
                ],
                axis=1,
            )
            both = jnp.concatenate([values, values * values], axis=0)
            operand = jnp.concatenate(split3(both), axis=0)
            split_ref[j, :, span] = operand
        wide_score = jnp.dot(weights, operand, preferred_element_type=f32)
        score = wide_score[:comps] + (
            wide_score[comps : 2 * comps] + wide_score[2 * comps : 3 * comps]
        )
        return operand, score

    pieces = [(j, first) for j in range(together) for first in range(0, cols, chunk)]
    ahead = scores(*pieces[0])
    moment = total[...]
    for index, (j, first) in enumerate(pieces):
        operand, score = ahead
        if index + 1 < len(pieces):
            ahead = scores(*pieces[index + 1])
        exponent = jnp.exp(score - jnp.max(score, axis=0, keepdims=True))
        share = exponent * (1.0 / jnp.sum(exponent, axis=0, keepdims=True))
        high = share.astype(bf16)
        low = (share - high.astype(f32)).astype(bf16)
        moment = moment + lax.dot_general(
            jnp.concatenate([high, low], axis=0),
            operand,
            (((1,), (1,)), ((), ())),
            preferred_element_type=f32,
        )
        if last:
            for y in range(chunk):
                wide[pl.ds((j * comps) * cols + first + y, comps, stride=cols), :] = share[
                    :, y * LANES : (y + 1) * LANES
                ]
    total[...] = moment
    if last:
        for j in range(together):
            for k in range(comps):
                start = (j * comps + k) * cols
                post_ref[j, k] = wide[start : start + cols, :].astype(bf16)

    @pl.when(step == pl.num_programs(0) - 1)
    def _():
        both = total[:comps] + total[comps:]
        both = jnp.concatenate([both, jnp.zeros((comps, 2 * LANES - 6 * pad), f32)], axis=1)
        summed = (
            both
            + pltpu.roll(both, 2 * LANES - 2 * pad, 1)
            + pltpu.roll(both, 2 * LANES - 4 * pad, 1)
        )[:, :LANES]
        lane = lax.broadcasted_iota(jnp.int32, (comps, LANES), 1)
        summed = jnp.where(lane < 2 * pad, summed, 0.0)
        half = comps // 2
        folded = summed[:half] + pltpu.roll(summed[half:], LANES // 2, 1)
        if last:
            moment_ref[...] = folded
        else:
            payload[...] = folded
            moment_ref[...] = gather_sum(inlines, xlines, payload, slots, send_sem, recv_sem)


def moments(features, split, summed, init, count, rows, cells):
    last = summed is not None
    inlines, xlines = lax.axis_size("inline"), lax.axis_size("xline")
    comps = init[0].shape[1]
    cols, flat, samples = features.shape
    pad = flat // rows
    assert 4 * pad <= LANES and comps % 16 == 0
    chunk = 4
    together = 2
    folded = jax.ShapeDtypeStruct((comps // 2, LANES), f32)
    inputs = ([summed] if last else []) + list(init)
    out_shape, out_specs = [folded], [pl.BlockSpec(folded.shape, lambda j: (0, 0))]
    split_shape = (rows, 6 * pad, cols * samples)
    split_spec = pl.BlockSpec((together,) + split_shape[1:], lambda j: (j, 0, 0))
    scratch = [
        pltpu.VMEM((3 * comps, 2 * LANES), bf16),
        pltpu.VMEM((2 * comps, 6 * pad), f32),
    ]
    params = dict(vmem_limit_bytes=24 << 20)
    if last:
        out_shape.append(jax.ShapeDtypeStruct((rows, comps, cols, samples), bf16))
        out_specs.append(pl.BlockSpec((together, comps, cols, samples), lambda j: (j, 0, 0, 0)))
        scratch.append(pltpu.VMEM((together * comps * cols, samples), f32))
    else:
        out_shape.append(jax.ShapeDtypeStruct(split_shape, bf16))
        out_specs.append(split_spec)
        scratch += [pltpu.VMEM((pad, LANES), f32), pltpu.VMEM(folded.shape, f32)]
        scratch += gather_scratch(inlines * xlines, comps)
        params.update(collective_id=1, has_side_effects=True)
    sizes = (cols, pad, count, chunk, together, cells, inlines, xlines)
    return pl.pallas_call(
        functools.partial(moment_kernel, sizes, last),
        out_shape=out_shape,
        grid=(rows // together,),
        in_specs=[split_spec if last else pl.BlockSpec(memory_space=VMEM)]
        + [pl.BlockSpec(array.shape, lambda j: (0, 0)) for array in inputs],
        out_specs=out_specs,
        scratch_shapes=scratch,
        compiler_params=pltpu.CompilerParams(**params),
        name="last_pass" if last else "first_pass",
    )(split if last else features, *inputs)


def sum_kernel(inlines, xlines, moment_ref, out_ref, slots, send_sem, recv_sem):
    greet(inlines, xlines)
    out_ref[...] = gather_sum(inlines, xlines, moment_ref, slots, send_sem, recv_sem)


def sum_moments(moment):
    inlines, xlines = lax.axis_size("inline"), lax.axis_size("xline")
    return pl.pallas_call(
        functools.partial(sum_kernel, inlines, xlines),
        out_shape=jax.ShapeDtypeStruct(moment.shape, f32),
        in_specs=[pl.BlockSpec(memory_space=VMEM)],
        out_specs=pl.BlockSpec(memory_space=VMEM),
        scratch_shapes=gather_scratch(inlines * xlines, 2 * moment.shape[0]),
        compiler_params=pltpu.CompilerParams(
            collective_id=2, has_side_effects=True, vmem_limit_bytes=4 << 20
        ),
        name="sum_moments",
    )(moment)


def final_kernel(sizes, *refs):
    *sums, mean_ref, var_ref, weight_ref, mean_out, var_out, weight_out = refs
    count = sizes[1]
    params, shift_row = first_params(mean_ref, var_ref, weight_ref)
    for summed in sums:
        params = next_params(summed[...], params, sizes)
    means, spreads, weights = params
    comps = means.shape[0]
    blank = jnp.zeros((LANES - comps, LANES), f32)
    turned = [
        jnp.transpose(jnp.concatenate([value, blank], axis=0))[:, :comps]
        for value in (means + shift_row, spreads, weights)
    ]
    mean_out[...] = turned[0][:count]
    var_out[...] = turned[1][:count]
    weight_out[...] = turned[2][:1]


def finish(sums, init, sizes):
    count, comps = init[0].shape
    inputs = sums + list(init)
    return pl.pallas_call(
        functools.partial(final_kernel, sizes),
        out_shape=[
            jax.ShapeDtypeStruct((count, comps), f32),
            jax.ShapeDtypeStruct((count, comps), f32),
            jax.ShapeDtypeStruct((1, comps), f32),
        ],
        in_specs=[pl.BlockSpec(memory_space=VMEM)] * len(inputs),
        out_specs=[pl.BlockSpec(memory_space=VMEM)] * 3,
        compiler_params=pltpu.CompilerParams(vmem_limit_bytes=4 << 20),
        name="finish",
    )(*inputs)


def per_device(traces, directions, init_means, init_variances, init_weights):
    rows, cols, samples = traces.shape
    assert samples == LANES and rows >= HALF and rows % 8 == 0 and cols % 4 == 0
    count = 2 * directions.shape[0]
    pad = round_up(count + 1, 8)
    comps = init_weights.shape[0]
    cells = lax.axis_size("inline") * rows * lax.axis_size("xline") * cols * samples
    init = (init_means.T, init_variances.T, init_weights.reshape(1, comps))
    halo = gather_halo(traces)
    features = filter_features(halo, directions, pad)
    summed, split = moments(features, None, None, init, count, rows, cells)
    moment, posterior = moments(features, split, summed, init, count, rows, cells)
    sums = [summed, sum_moments(moment)]
    means, spreads, weights = finish(sums, init, (pad, count, cells))
    return posterior, means.T, spreads.T, weights.reshape(comps)


def solution(mesh):
    in_specs = (P(("slab", "inline"), "xline", None), P(), P(), P(), P())
    out_specs = (
        P(("slab", "inline"), None, "xline", None),
        P("slab", None),
        P("slab", None),
        P("slab"),
    )
    return jax.shard_map(
        per_device, mesh=mesh, in_specs=in_specs, out_specs=out_specs, check_vma=False
    )
```

profile of v0, /device:TPU:0, one launch (start us, length us, event | category | flops | bytes accessed | tf_op | source)
XLA Modules:
  0.0 72.6 jit_solution(10874470299792201719)
XLA Ops:
  0.6 0.0 copy-start.1
  0.6 0.0 copy-start
  0.7 0.0 copy-start.2
  0.7 0.9 %copy-done.2 = bf16[16,24,128]{2,1,0:T(8,128)(2,1)S(1)} copy-done((bf16[16,24,128]{2,1,0:T(8,128)(2,1)S(1)}, bf16[16,24,128]{2,1,0:T(8,128)(2,1)}, u32[]{:S(2)}) %copy-start.2) | copy-done | bytes 98328
  1.6 0.0 copy-start.3
  1.6 8.2 %halo.1.halo_ref = bf16[3,2,16,24,128]{4,3,2,1,0:T(8,128)(2,1)S(1)} custom-call(bf16[16,24,128]{2,1,0:T(8,128)(2,1)S(1)} %copy-done.2), custom_call_target="tpu_custom_call" | custom-call | tf_op jit(solution)/shard_map/halo/pallas_call | solution.py:107
  9.7 0.0 copy-start.4
  9.7 0.6 copy-done.4
  10.4 20.5 %filters.1.refs_0_ = f32[24,384,128]{2,1,0:T(8,128)S(1)} custom-call(s32[10]{0:T(128)S(1)} %copy-done.4, bf16[3,2,16,24,128]{4,3,2,1,0:T(8,128)(2,1)S(1)} %halo.1.halo_ref), custom_call_target="tpu_custom_call" | custom-call | tf_op jit(solution)/shard_map/filters/pallas_call | solution.py:257
  30.9 0.0 copy-done.1
  30.9 0.0 copy-done
  30.9 0.0 copy-done.3
  30.9 19.7 %first_pass.1 = (f32[16,128]{1,0:T(8,128)S(1)}, bf16[16,144,3072]{2,1,0:T(8,128)(2,1)S(1)}) custom-call(f32[24,384,128]{2,1,0:T(8,128)S(1)} %filters.1.refs_0_, f32[20,32]{1,0:T(8,128)S(1)} %bitcast.6, f32[20,32]{1,0:T(8,128)S(1)} %bitcast.9, f32[1,32]{1,0:T(1,128)S(1)} %bitcast.12), custom_call_target="tpu_custom_call" | custom-call | tf_op jit(solution)/shard_map/first_pass/pallas_call | solution.py:506
  50.7 13.2 %last_pass.1 = (f32[16,128]{1,0:T(8,128)S(1)}, bf16[16,32,24,128]{3,2,1,0:T(8,128)(2,1)}) custom-call(bf16[16,144,3072]{2,1,0:T(8,128)(2,1)S(1)} %get-tuple-element.11.refs_0_, f32[16,128]{1,0:T(8,128)S(1)} %get-tuple-element.12.refs_1_.refs_0_, f32[20,32]{1,0:T(8,128)S(1)} %bitcast.7, f32[20,32]{1,0:T(8,128)S(1)} %bitcast.10, f32[1,32]{1,0:T(1,128)S(1)} %bitcast.13), custom_call_target="tpu_custom_call" | custom-call | tf_op jit(solution)/shard_map/last_pass/pallas_call | solution.py:506
  63.8 7.9 %sum_moments.1.refs_1_ = f32[16,128]{1,0:T(8,128)S(1)} custom-call(f32[16,128]{1,0:T(8,128)S(1)} %get-tuple-element.14.moment_ref), custom_call_target="tpu_custom_call" | custom-call | tf_op jit(solution)/shard_map/sum_moments/pallas_call | solution.py:526
  71.8 0.8 %finish.1 = (f32[20,32]{1,0:T(8,128)}, f32[20,32]{1,0:T(8,128)}, f32[1,32]{1,0:T(1,128)}) custom-call(f32[16,128]{1,0:T(8,128)S(1)} %get-tuple-element.12.refs_1_.refs_0_, f32[16,128]{1,0:T(8,128)S(1)} %sum_moments.1.refs_1_, f32[20,32]{1,0:T(8,128)S(1)} %bitcast.8, f32[20,32]{1,0:T(8,128)S(1)} %bitcast.11, f32[1,32]{1,0:T(1,128)S(1)} %bitcast.14), custom_call_target="tpu_custom_call" | custom-call | tf_op jit(solution)/shard_map/finish/pallas_call | solution.py:560
Async XLA Ops:
  0.6 30.3 %copy-start.1 = (f32[32,20]{0,1:T(8,128)S(1)}, f32[32,20]{0,1:T(8,128)}, u32[]{:S(2)}) copy-start(f32[32,20]{0,1:T(8,128)} %param.8) | copy-start | bytes 7684
  0.6 30.3 %copy-start = (f32[32,20]{0,1:T(8,128)S(1)}, f32[32,20]{0,1:T(8,128)}, u32[]{:S(2)}) copy-start(f32[32,20]{0,1:T(8,128)} %param.7) | copy-start | bytes 7684
  0.7 0.9 %copy-start.2 = (bf16[16,24,128]{2,1,0:T(8,128)(2,1)S(1)}, bf16[16,24,128]{2,1,0:T(8,128)(2,1)}, u32[]{:S(2)}) copy-start(bf16[16,24,128]{2,1,0:T(8,128)(2,1)} %own_ref.1) | copy-start | bytes 294916
  1.6 29.4 %copy-start.3 = (f32[32]{0:T(128)S(1)}, f32[32]{0:T(128)}, u32[]{:S(2)}) copy-start(f32[32]{0:T(128)} %param.9) | copy-start | bytes 388
  9.7 0.7 copy-start.4
where the time goes:
time: 72.8 us; the launch traced here: 72.6 us
  Pallas kernels  70.3 us (97%)
  local copies, waits for them, and re-layouts  1.56 us (2%)
    pallas_call x2, Pallas kernels, moments(): pl.pallas_call(functools.partial(moment_kernel, sizes, last), out_shape=o...  32.9 us
    pallas_call x1, Pallas kernels, filter_features(): pl.pallas_call(functools.partial(filter_kernel, sizes), out_shape=jax.Sha...  20.5 us
    pallas_call x1, Pallas kernels, gather_halo(): pl.pallas_call(functools.partial(halo_kernel, inlines, xlines), out_shape...  8.16 us
    pallas_call x1, Pallas kernels, sum_moments(): pl.pallas_call(functools.partial(sum_kernel, inlines, xlines), out_shape=...  7.93 us
    unnamed x10, local copies, waits for them, and re-layouts  1.56 us

commit v1 on v0

--- a/solution.py
+++ b/solution.py
@@ -31,9 +31,91 @@
     return -(-value // step) * step
 
 
-def halo_kernel(inlines, xlines, own_ref, out_ref, send_sem, recv_sem):
+def iotas(shape):
+    return (
+        lax.broadcasted_iota(jnp.int32, shape, 0),
+        lax.broadcasted_iota(jnp.int32, shape, 1),
+    )
+
+
+def roll(value, amount):
+    return value if amount == 0 else pltpu.roll(value, amount, 1)
+
+
+def taps(wave, difference):
+    offset = (difference - HALF).astype(f32)
+    wave = jnp.concatenate([wave] * (difference.shape[1] // LANES), axis=1)
+    wave = jnp.concatenate([wave] * (difference.shape[0] // 8), axis=0)
+    phase = offset * wave
+    envelope = jnp.exp(-offset * offset / (2.0 * width_scale * width_scale)) / norm
+    hit = jnp.logical_and(difference >= 0, difference < TAPS)
+    real = jnp.where(hit, envelope * jnp.cos(phase), 0.0)
+    imag = jnp.where(hit, envelope * jnp.sin(phase), 0.0)
+    return real, imag
+
+
+def angle(value, step):
+    return jnp.full((8, LANES), value.astype(f32)) * step
+
+
+def time_table(dip, time_ref):
+    wave = wavenumber * jnp.cos(angle(dip + 1, math.pi / (2 * DIPS + 2)))
+    sub, lane = iotas((8, LANES))
+    bases = taps(wave, jnp.bitwise_and(sub - lane + HALF, LANES - 1))
+    for s in range(0, LANES, 16):
+        pieces = []
+        for start in (s, s + 8):
+            near = jnp.abs(sub + start - lane) <= HALF
+            pieces.append(
+                jnp.concatenate([jnp.where(near, roll(base, start), 0.0) for base in bases], axis=1)
+            )
+        time_ref[dip, s : s + 16, :] = jnp.concatenate(pieces, axis=0).astype(bf16)
+
+
+def space_tables(orient, direction, sizes, col, x_ref, i_ref):
+    rows, cols, width, group = sizes
+    lanes = 2 * LANES
+    azimuth = angle(direction % AZIMUTHS, math.pi / AZIMUTHS)
+    dip_angle = angle(direction // AZIMUTHS + 1, math.pi / (2 * DIPS + 2))
+    inline_wave = wavenumber * (jnp.sin(dip_angle) * jnp.cos(azimuth))
+    xline_wave = wavenumber * (jnp.sin(dip_angle) * jnp.sin(azimuth))
+
+    sub, lane = iotas((8, lanes))
+    row, step = sub % group, sub // group
+    place = jnp.where(lane >= group * width, lane - lanes, lane)
+    bases = taps(xline_wave, place - row * width - step - col * cols + HALF)
+    mine = jnp.logical_and(lane >= row * width, lane < (row + 1) * width)
+    per = 8 // group
+    for part in range(2):
+        for y in range(0, cols, 2 * per):
+            pair = jnp.concatenate(
+                [jnp.where(mine, roll(bases[part], y + dy), 0.0) for dy in (0, per)], axis=0
+            )
+            start = (part * cols + y) * group
+            x_ref[orient, start : start + 16, :] = pair[:, : group * width].astype(bf16)
+
+    deep = 3 * rows
+    half = per * deep
+    sub, lane = iotas((rows, lanes))
+    imag_in = lane >= half
+    within = jnp.where(imag_in, lane - half, lane)
+    line = (within // 8) * group + within % group
+    step = (within // group) % per
+    real, imag = taps(inline_wave, line - sub - rows + HALF)
+    blocks = [jnp.where(imag_in, -imag, real), jnp.where(imag_in, real, imag)]
+    for dy in range(per):
+        for index, block in enumerate(blocks):
+            start = (dy * 2 + index) * rows
+            value = jnp.where(step == dy, block, 0.0)
+            i_ref[orient, start : start + rows, :] = value[:, : 2 * half].astype(bf16)
+
+
+def halo_kernel(inlines, xlines, sizes, dir_ref, own_ref, out_ref, time_ref, x_ref, i_ref, *sems):
+    send_sem, recv_sem, own_sem = sems
     row = lax.axis_index("inline")
     col = lax.axis_index("xline")
+    cols = sizes[1]
+    mine = pl.ds(pl.multiple_of(col * cols, 8), cols)
 
     def there(side):
         return row > 0 if side < 0 else row < inlines - 1
@@ -52,13 +134,20 @@
             device_id={"xline": lax.rem(col + shift, xlines)},
             device_id_type=MESH,
         )
+    own = pltpu.make_async_copy(own_ref, out_ref.at[1, :, mine], own_sem.at[0])
+    own.start()
+
+    @pl.loop(0, DIPS)
+    def _(dip):
+        time_table(dip, time_ref)
+
     sides = (row > 0).astype(jnp.int32) + (row < inlines - 1).astype(jnp.int32)
     pl.semaphore_wait(barrier, sides + xlines - 1)
 
     def along(side):
         return pltpu.make_async_remote_copy(
             src_ref=own_ref,
-            dst_ref=out_ref.at[1 - side, col],
+            dst_ref=out_ref.at[1 - side, :, mine],
             send_sem=send_sem.at[1 - side, 0],
             recv_sem=recv_sem.at[1 - side, 0],
             device_id={"inline": row + side},
@@ -67,8 +156,8 @@
 
     def across(block, shift):
         return pltpu.make_async_remote_copy(
-            src_ref=own_ref if block == 1 else out_ref.at[block, col],
-            dst_ref=out_ref.at[block, col],
+            src_ref=own_ref if block == 1 else out_ref.at[block, :, mine],
+            dst_ref=out_ref.at[block, :, mine],
             send_sem=send_sem.at[block, shift],
             recv_sem=recv_sem.at[block, shift],
             device_id={"xline": lax.rem(col + shift, xlines)},
@@ -81,17 +170,30 @@
             along(side).start()
     for shift in range(1, xlines):
         across(1, shift).start()
-    out_ref[1, col] = own_ref[...]
     for side in (-1, 1):
         @pl.when(jnp.logical_not(there(side)))
         def _(side=side):
             out_ref[1 + side] = jnp.zeros(out_ref.shape[1:], out_ref.dtype)
+
+    orients = x_ref.shape[0]
+    early = orients // 2
+
+    @pl.loop(0, early)
+    def _(orient):
+        space_tables(orient, dir_ref[orient], sizes, col, x_ref, i_ref)
+
     for side in (-1, 1):
         @pl.when(there(side))
         def _(side=side):
             along(-side).wait_recv()
             for shift in range(1, xlines):
                 across(1 + side, shift).start()
+
+    @pl.loop(early, orients)
+    def _(orient):
+        space_tables(orient, dir_ref[orient], sizes, col, x_ref, i_ref)
+
+    own.wait()
     for shift in range(1, xlines):
         across(1, shift).wait()
     for side in (-1, 1):
@@ -102,175 +204,131 @@
                 across(1 + side, shift).wait()
 
 
-def gather_halo(traces):
+def gather_halo(traces, directions):
     inlines, xlines = lax.axis_size("inline"), lax.axis_size("xline")
+    rows, cols, samples = traces.shape
+    orients = directions.shape[0]
+    width = xlines * cols
+    group = 4
+    assert group * width + cols <= 2 * LANES
+    per = 8 // group
+    sizes = (rows, cols, width, group)
     return pl.pallas_call(
-        functools.partial(halo_kernel, inlines, xlines),
-        out_shape=jax.ShapeDtypeStruct((3, xlines) + traces.shape, traces.dtype),
-        in_specs=[pl.BlockSpec(memory_space=VMEM)],
-        out_specs=pl.BlockSpec(memory_space=VMEM),
+        functools.partial(halo_kernel, inlines, xlines, sizes),
+        out_shape=[
+            jax.ShapeDtypeStruct((3, rows, width, samples), traces.dtype),
+            jax.ShapeDtypeStruct((DIPS, samples, 2 * samples), bf16),
+            jax.ShapeDtypeStruct((orients, 2 * cols * group, group * width), bf16),
+            jax.ShapeDtypeStruct((orients, 2 * per * rows, 2 * per * 3 * rows), bf16),
+        ],
+        in_specs=[pl.BlockSpec(memory_space=SMEM), pl.BlockSpec(memory_space=pl.ANY)],
+        out_specs=[pl.BlockSpec(memory_space=VMEM)] * 4,
         scratch_shapes=[
             pltpu.SemaphoreType.DMA((3, xlines)),
             pltpu.SemaphoreType.DMA((3, xlines)),
+            pltpu.SemaphoreType.DMA((1,)),
         ],
         compiler_params=pltpu.CompilerParams(
-            collective_id=0, has_side_effects=True, vmem_limit_bytes=4 << 20
+            collective_id=0, has_side_effects=True, vmem_limit_bytes=8 << 20
         ),
         name="halo",
-    )(traces)
-
-
-def filter_kernel(sizes, dir_ref, halo_ref, out_ref, flat, x_mat, cross):
-    rows, cols, width, pad, orients = sizes
+    )(directions, traces)
+
+
+def filter_kernel(sizes, dir_ref, halo_ref, time_ref, x_ref, i_ref, out_ref, band, cross):
+    rows, cols, width, pad, orients, group = sizes
+    per = 8 // group
     deep = 3 * rows
-    group = 8
-    orient = pl.program_id(0)
-
-    @pl.when(orient == 0)
-    def _():
-        for block in range(3):
-            for i in range(rows):
-                for part in range(width // cols):
-                    start = ((block * rows + i) * width) + part * cols
-                    flat[start : start + cols, :] = halo_ref[block, part, i]
-        for y in range(cols):
-            for extra in range(pad - 2 * orients):
-                out_ref[y, pl.ds(2 * orients + extra, rows, stride=pad), :] = jnp.full(
-                    (rows, LANES), 1.0 if extra == 0 else 0.0, f32
-                )
-
-    direction = dir_ref[orient]
-    azimuth = jnp.full((8, LANES), (direction % AZIMUTHS).astype(f32)) * (math.pi / AZIMUTHS)
-    dip_angle = jnp.full((8, LANES), (direction // AZIMUTHS + 1).astype(f32)) * (
-        math.pi / (2 * DIPS + 2)
-    )
-    waves = [
-        wavenumber * (jnp.sin(dip_angle) * jnp.cos(azimuth)),
-        wavenumber * (jnp.sin(dip_angle) * jnp.sin(azimuth)),
-        wavenumber * jnp.cos(dip_angle),
-    ]
-
-    def toeplitz(axis, difference):
-        offset = (difference - HALF).astype(f32)
-        copies = difference.shape[1] // LANES
-        wave = waves[axis]
-        phase = offset * (wave if copies == 1 else jnp.concatenate([wave] * copies, axis=1))
-        envelope = jnp.exp(-offset * offset / (2.0 * width_scale * width_scale)) / norm
-        hit = jnp.logical_and(difference >= 0, difference < TAPS)
-        real = jnp.where(hit, envelope * jnp.cos(phase), 0.0)
-        imag = jnp.where(hit, envelope * jnp.sin(phase), 0.0)
-        return real, imag
-
-    def iotas(shape):
-        return (
-            lax.broadcasted_iota(jnp.int32, shape, 0),
-            lax.broadcasted_iota(jnp.int32, shape, 1),
-        )
-
-    def roll(value, amount):
-        return value if amount == 0 else pltpu.roll(value, amount, 1)
-
-    sub, lane = iotas((8, LANES))
-    bases = toeplitz(2, jnp.bitwise_and(sub - lane + HALF, LANES - 1))
-    pieces = []
-    for s in range(0, LANES, 8):
-        near = jnp.abs(sub + s - lane) <= HALF
-        pieces.append(
-            jnp.concatenate([jnp.where(near, roll(base, s), 0.0) for base in bases], axis=1)
-        )
-    time_mat = jnp.concatenate(pieces, axis=0).astype(bf16)
-
-    lanes = round_up(group * width + LANES, LANES)
-    sub, lane = iotas((group, lanes))
-    difference = lane - sub * width - lax.axis_index("xline") * cols + HALF
-    bases = toeplitz(1, jnp.where(difference >= lanes - 64, difference - lanes, difference))
-    mine = jnp.logical_and(lane >= sub * width, lane < (sub + 1) * width)
-    for part in range(2):
-        for y in range(0, cols, 2):
-            pair = jnp.concatenate(
-                [jnp.where(mine, roll(bases[part], y + dy), 0.0) for dy in range(2)], axis=0
+    half = per * deep
+    span = group * width
+    pairs = cols // per
+    block = rows * width
+
+    for y in range(cols):
+        for extra in range(pad - 2 * orients):
+            out_ref[y, pl.ds(2 * orients + extra, rows, stride=pad), :] = jnp.full(
+                (rows, LANES), 1.0 if extra == 0 else 0.0, f32
             )
-            start = (part * cols + y) * group
-            x_mat[start : start + 2 * group, :] = pair[:, : group * width].astype(bf16)
-
-    sub, lane = iotas((8, LANES))
-    bases = toeplitz(0, jnp.bitwise_and(lane - sub - rows + HALF, LANES - 1))
-    real_first, imag_first = [
-        jnp.concatenate(
-            [jnp.where(lane < deep, roll(base, j), 0.0) for j in range(0, rows, 8)], axis=0
-        )
-        for base in bases
-    ]
-    blank = jnp.zeros((rows, LANES), f32)
-    real_first, imag_first = [
-        jnp.concatenate([part, blank], axis=1) for part in (real_first, imag_first)
-    ]
-    real_next, imag_next = pltpu.roll(real_first, deep, 1), pltpu.roll(imag_first, deep, 1)
-    base = jnp.concatenate([real_first - imag_next, imag_first + real_next], axis=0)
-    i_mat = jnp.concatenate([base, pltpu.roll(base, 2 * deep, 1)], axis=0).astype(bf16)
-    i_mat = i_mat[:, : 4 * deep]
-
-    for step in range(deep // group):
-        span = group * width
-        band = jnp.dot(
-            flat[step * span : (step + 1) * span, :],
-            time_mat,
-            preferred_element_type=f32,
-        ).astype(bf16)
-        mixed = jnp.dot(x_mat[...], band, preferred_element_type=f32)
-        for y in range(cols):
-            with_cos = mixed[y * group : (y + 1) * group]
-            with_sin = mixed[(cols + y) * group : (cols + y + 1) * group]
-            cu, cv = with_cos[:, :LANES], with_cos[:, LANES:]
-            su, sv = with_sin[:, :LANES], with_sin[:, LANES:]
-            for slot, value in enumerate((cu - sv, su + cv, cu + sv, su - cv)):
-                start = (slot * cols + y) * deep + step * group
-                cross[start : start + group, :] = value
-
-    half = cols // 2
-    for q in range(2):
-        for y0 in range(0, half, 2):
-            columns = []
-            for dy in range(2):
-                pieces = []
-                for g in range(2):
-                    for r in range(2):
-                        start = ((q * 2 + r) * cols + y0 + dy + g * half) * deep
-                        pieces.append(cross[start : start + deep, :])
-                columns.append(jnp.concatenate(pieces, axis=0).astype(bf16))
-            total = jnp.dot(i_mat, jnp.concatenate(columns, axis=1), preferred_element_type=f32)
-            for g in range(2):
-                re = total[g * 2 * rows : g * 2 * rows + rows]
-                im = total[g * 2 * rows + rows : (g + 1) * 2 * rows]
-                size = jnp.sqrt(re * re + im * im + eps_mag)
-                for dy in range(2):
-                    out_ref[
-                        y0 + dy + g * half, pl.ds(2 * orient + q, rows, stride=pad), :
-                    ] = size[:, dy * LANES : (dy + 1) * LANES]
-
-
-def filter_features(halo, directions, pad):
-    _, xlines, rows, cols, samples = halo.shape
-    orients = directions.shape[0]
-    width = xlines * cols
-    sizes = (rows, cols, width, pad, orients)
+
+    @pl.loop(0, DIPS)
+    def _(dip):
+        for b in range(3):
+            lines = halo_ref[b].reshape(block, LANES)
+            band[dip, b * block : (b + 1) * block, :] = jnp.dot(
+                lines, time_ref[dip], preferred_element_type=f32
+            ).astype(bf16)
+
+    def across(orient, dip, step):
+        mixed = [
+            jnp.dot(
+                x_ref[orient],
+                band[dip, (2 * step + h) * span : (2 * step + h + 1) * span, :],
+                preferred_element_type=f32,
+            )
+            for h in range(2)
+        ]
+        for yp in range(pairs):
+            slots = [[], [], [], []]
+            for h in range(2):
+                with_cos = mixed[h][yp * 8 : (yp + 1) * 8]
+                with_sin = mixed[h][(pairs + yp) * 8 : (pairs + yp + 1) * 8]
+                cu, cv = with_cos[:, :LANES], with_cos[:, LANES:]
+                su, sv = with_sin[:, :LANES], with_sin[:, LANES:]
+                for slot, value in zip(slots, (cu - sv, su + cv, cu + sv, su - cv)):
+                    slot.append(value)
+            for index, slot in enumerate(slots):
+                q, r = index // 2, index % 2
+                start = ((q * pairs + yp) * 2 + r) * half + step * 16
+                cross[start : start + 16, :] = jnp.concatenate(slot, axis=0).astype(bf16)
+
+    def along(orient, q, j):
+        start = (q * pairs + 2 * j) * 2 * half
+        operand = jnp.concatenate(
+            [
+                cross[start : start + 2 * half, :],
+                cross[start + 2 * half : start + 4 * half, :],
+            ],
+            axis=1,
+        )
+        total = jnp.dot(i_ref[orient], operand, preferred_element_type=f32)
+        for dy in range(per):
+            re = total[(2 * dy) * rows : (2 * dy + 1) * rows]
+            im = total[(2 * dy + 1) * rows : (2 * dy + 2) * rows]
+            square = re * re + im * im + eps_mag
+            size = square * lax.rsqrt(square)
+            for h in range(2):
+                out_ref[
+                    (2 * j + h) * per + dy, pl.ds(2 * orient + q, rows, stride=pad), :
+                ] = size[:, h * LANES : (h + 1) * LANES]
+
+    @pl.loop(0, orients)
+    def _(orient):
+        dip = dir_ref[orient] // AZIMUTHS
+        for step in range(deep // (2 * group)):
+            across(orient, dip, step)
+        for q in range(2):
+            for j in range(pairs // 2):
+                along(orient, q, j)
+
+
+def filter_features(halo, tables, directions, pad):
+    _, rows, width, samples = halo.shape
+    orients, height, depth = tables[1].shape
+    group = depth // width
+    cols = height // (2 * group)
+    sizes = (rows, cols, width, pad, orients, group)
     return pl.pallas_call(
         functools.partial(filter_kernel, sizes),
         out_shape=jax.ShapeDtypeStruct((cols, rows * pad, samples), f32),
-        grid=(orients,),
-        in_specs=[
-            pl.BlockSpec(memory_space=SMEM),
-            pl.BlockSpec(memory_space=VMEM),
-        ],
+        in_specs=[pl.BlockSpec(memory_space=SMEM)] + [pl.BlockSpec(memory_space=VMEM)] * 4,
         out_specs=pl.BlockSpec(memory_space=VMEM),
         scratch_shapes=[
-            pltpu.VMEM((3 * rows * width, samples), bf16),
-            pltpu.VMEM((2 * cols * 8, 8 * width), bf16),
-            pltpu.VMEM((4 * cols * 3 * rows, samples), f32),
+            pltpu.VMEM((DIPS, 3 * rows * width, 2 * samples), bf16),
+            pltpu.VMEM((4 * cols * 3 * rows, samples), bf16),
         ],
-        compiler_params=pltpu.CompilerParams(vmem_limit_bytes=20 << 20),
+        compiler_params=pltpu.CompilerParams(vmem_limit_bytes=24 << 20),
         name="filters",
-    )(directions, halo)
+    )(directions, halo, *tables)
 
 
 def split3(value):
@@ -579,8 +637,8 @@
     comps = init_weights.shape[0]
     cells = lax.axis_size("inline") * rows * lax.axis_size("xline") * cols * samples
     init = (init_means.T, init_variances.T, init_weights.reshape(1, comps))
-    halo = gather_halo(traces)
-    features = filter_features(halo, directions, pad)
+    halo, *tables = gather_halo(traces, directions)
+    features = filter_features(halo, tables, directions, pad)
     summed, split = moments(features, None, None, init, count, rows, cells)
     moment, posterior = moments(features, split, summed, init, count, rows, cells)
     sums = [summed, sum_moments(moment)]

time: 72.8 us -> 64.1 us (0.88)
  Pallas kernels: 70.3 us -> 61 us
    pallas_call x1, Pallas kernels: 20.5 us -> 10.7 us  [filter_features(): pl.pallas_call(functools.partial(filter_kernel, sizes), out_shape=jax.Sha...]
    pallas_call x1, Pallas kernels: 8.16 us -> 8.92 us  [gather_halo(): pl.pallas_call(functools.partial(halo_kernel, inlines, xlines, sizes), ou...]
    unnamed x10 -> x12, local copies, waits for them, and re-layouts: 1.56 us -> 2.21 us
where the time goes in v1:
time: 64.1 us; the launch traced here: 64 us
  Pallas kernels  61 us (95%)
  local copies, waits for them, and re-layouts  2.21 us (3%)
  between operations  0.72 us (1%)
    pallas_call x2, Pallas kernels, moments(): pl.pallas_call(functools.partial(moment_kernel, sizes, last), out_shape=o...  32.9 us
    pallas_call x1, Pallas kernels, filter_features(): pl.pallas_call(functools.partial(filter_kernel, sizes), out_shape=jax.Sha...  10.7 us
    pallas_call x1, Pallas kernels, gather_halo(): pl.pallas_call(functools.partial(halo_kernel, inlines, xlines, sizes), ou...  8.92 us
    pallas_call x1, Pallas kernels, sum_moments(): pl.pallas_call(functools.partial(sum_kernel, inlines, xlines), out_shape=...  7.6 us
    unnamed x12, local copies, waits for them, and re-layouts  2.21 us

profile of v1, /device:TPU:0, one launch (start us, length us, event | category | flops | bytes accessed | tf_op | source)
XLA Modules:
  0.0 64.0 jit_solution(14345577851385770412)
XLA Ops:
  0.6 0.0 copy-start.1
  0.6 0.0 copy-start
  0.7 0.0 copy-start.2
  0.7 0.9 %copy-done.2 = bf16[16,24,128]{2,1,0:T(8,128)(2,1)S(1)} copy-done((bf16[16,24,128]{2,1,0:T(8,128)(2,1)S(1)}, bf16[16,24,128]{2,1,0:T(8,128)(2,1)}, u32[]{:S(2)}) %copy-start.2) | copy-done | bytes 98328
  1.6 0.0 copy-start.4
  1.6 0.7 %copy-done.4 = s32[10]{0:T(128)S(1)} copy-done((s32[10]{0:T(128)S(1)}, s32[10]{0:T(128)}, u32[]{:S(2)}) %copy-start.4) | copy-done | bytes 64
  2.2 0.0 copy-start.3
  2.2 8.9 %halo.1 = (bf16[3,16,48,128]{3,2,1,0:T(8,128)(2,1)S(1)}, bf16[4,128,256]{2,1,0:T(8,128)(2,1)S(1)}, bf16[10,192,192]{2,1,0:T(8,128)(2,1)S(1)}, bf16[10,64,192]{2,1,0:T(8,128)(2,1)S(1)}) custom-call(s32[10]{0:T(128)S(1)} %copy-done.4, bf16[16,24,128]{2,1,0:T(8,128)(2,1)S(1)} %copy-done.2), custom_call_target="tpu_custom_call" | custom-call | tf_op jit(solution)/shard_map/halo/pallas_call | solution.py:216
  11.1 0.0 copy-start.5
  11.2 0.6 %copy-done.5 = s32[10]{0:T(128)S(1)} copy-done((s32[10]{0:T(128)S(1)}, s32[10]{0:T(128)}, u32[]{:S(2)}) %copy-start.5) | copy-done | bytes 64
  11.8 10.7 %filters.1.refs_0_ = f32[24,384,128]{2,1,0:T(8,128)S(1)} custom-call(s32[10]{0:T(128)S(1)} %copy-done.5, bf16[3,16,48,128]{3,2,1,0:T(8,128)(2,1)S(1)} %get-tuple-element.15.halo_ref, bf16[4,128,256]{2,1,0:T(8,128)(2,1)S(1)} %get-tuple-element.16.time_ref, bf16[10,192,192]{2,1,0:T(8,128)(2,1)S(1)} %get-tuple-element.17.x_ref, ...), custom_call_target="tpu_custom_call" | custom-call | tf_op jit(solution)/shard_map/filters/pallas_call | solution.py:320
  22.5 0.0 copy-done.1
  22.5 0.0 copy-done
  22.6 0.0 copy-done.3
  22.6 19.8 %first_pass.1 = (f32[16,128]{1,0:T(8,128)S(1)}, bf16[16,144,3072]{2,1,0:T(8,128)(2,1)S(1)}) custom-call(f32[24,384,128]{2,1,0:T(8,128)S(1)} %filters.1.refs_0_, f32[20,32]{1,0:T(8,128)S(1)} %bitcast.6, f32[20,32]{1,0:T(8,128)S(1)} %bitcast.9, f32[1,32]{1,0:T(1,128)S(1)} %bitcast.12), custom_call_target="tpu_custom_call" | custom-call | tf_op jit(solution)/shard_map/first_pass/pallas_call | solution.py:564
  42.3 13.2 %last_pass.1 = (f32[16,128]{1,0:T(8,128)S(1)}, bf16[16,32,24,128]{3,2,1,0:T(8,128)(2,1)}) custom-call(bf16[16,144,3072]{2,1,0:T(8,128)(2,1)S(1)} %get-tuple-element.19.refs_0_, f32[16,128]{1,0:T(8,128)S(1)} %get-tuple-element.20.refs_1_.refs_0_, f32[20,32]{1,0:T(8,128)S(1)} %bitcast.7, f32[20,32]{1,0:T(8,128)S(1)} %bitcast.10, f32[1,32]{1,0:T(1,128)S(1)} %bitcast.13), custom_call_target="tpu_custom_call" | custom-call | tf_op jit(solution)/shard_map/last_pass/pallas_call | solution.py:564
  55.5 7.6 %sum_moments.1.refs_1_ = f32[16,128]{1,0:T(8,128)S(1)} custom-call(f32[16,128]{1,0:T(8,128)S(1)} %get-tuple-element.22.moment_ref), custom_call_target="tpu_custom_call" | custom-call | tf_op jit(solution)/shard_map/sum_moments/pallas_call | solution.py:584
  63.1 0.8 %finish.1 = (f32[20,32]{1,0:T(8,128)}, f32[20,32]{1,0:T(8,128)}, f32[1,32]{1,0:T(1,128)}) custom-call(f32[16,128]{1,0:T(8,128)S(1)} %get-tuple-element.20.refs_1_.refs_0_, f32[16,128]{1,0:T(8,128)S(1)} %sum_moments.1.refs_1_, f32[20,32]{1,0:T(8,128)S(1)} %bitcast.8, f32[20,32]{1,0:T(8,128)S(1)} %bitcast.11, f32[1,32]{1,0:T(1,128)S(1)} %bitcast.14), custom_call_target="tpu_custom_call" | custom-call | tf_op jit(solution)/shard_map/finish/pallas_call | solution.py:618
Async XLA Ops:
  0.6 21.9 %copy-start.1 = (f32[32,20]{0,1:T(8,128)S(1)}, f32[32,20]{0,1:T(8,128)}, u32[]{:S(2)}) copy-start(f32[32,20]{0,1:T(8,128)} %param.8) | copy-start | bytes 7684
  0.6 21.9 %copy-start = (f32[32,20]{0,1:T(8,128)S(1)}, f32[32,20]{0,1:T(8,128)}, u32[]{:S(2)}) copy-start(f32[32,20]{0,1:T(8,128)} %param.7) | copy-start | bytes 7684
  0.7 0.9 %copy-start.2 = (bf16[16,24,128]{2,1,0:T(8,128)(2,1)S(1)}, bf16[16,24,128]{2,1,0:T(8,128)(2,1)}, u32[]{:S(2)}) copy-start(bf16[16,24,128]{2,1,0:T(8,128)(2,1)} %own_ref.1) | copy-start | bytes 294916
  1.6 0.7 %copy-start.4 = (s32[10]{0:T(128)S(1)}, s32[10]{0:T(128)}, u32[]{:S(2)}) copy-start(s32[10]{0:T(128)} %dir_ref.3) | copy-start | bytes 124
  2.2 20.3 %copy-start.3 = (f32[32]{0:T(128)S(1)}, f32[32]{0:T(128)}, u32[]{:S(2)}) copy-start(f32[32]{0:T(128)} %param.9) | copy-start | bytes 388
  11.1 0.7 %copy-start.5 = (s32[10]{0:T(128)S(1)}, s32[10]{0:T(128)}, u32[]{:S(2)}) copy-start(s32[10]{0:T(128)} %dir_ref.3) | copy-start | bytes 124

commit v2 on v1

--- a/solution.py
+++ b/solution.py
@@ -21,6 +21,7 @@
     sum(math.exp(-n * n / (width_scale * width_scale)) for n in range(-HALF, HALF + 1))
 )
 MESH = pl.DeviceIdType.MESH
+LOG2E = math.log2(math.e)
 f32 = jnp.float32
 bf16 = jnp.bfloat16
 VMEM = pltpu.MemorySpace.VMEM
@@ -452,7 +453,7 @@
         constant = jnp.log(params[2][:, :1]) - 0.5 * jnp.sum(terms, axis=1, keepdims=True)
         row = jnp.where(used, scaled, 0.0) + jnp.where(lane == count, constant, 0.0)
         row = row + pltpu.roll(-0.5 * inverse, pad, 1)
-        parts = split3(row)
+        parts = split3(row * LOG2E)
         for index, part in enumerate(parts):
             part = part.astype(f32)
             tiled = part + pltpu.roll(part, 2 * pad, 1) + pltpu.roll(part, 4 * pad, 1)
@@ -489,13 +490,13 @@
         operand, score = ahead
         if index + 1 < len(pieces):
             ahead = scores(*pieces[index + 1])
-        exponent = jnp.exp(score - jnp.max(score, axis=0, keepdims=True))
+        exponent = jnp.exp2(score - jnp.max(score, axis=0, keepdims=True))
         share = exponent * (1.0 / jnp.sum(exponent, axis=0, keepdims=True))
         high = share.astype(bf16)
         low = (share - high.astype(f32)).astype(bf16)
         moment = moment + lax.dot_general(
             jnp.concatenate([high, low], axis=0),
-            operand,
+            operand[: 4 * pad],
             (((1,), (1,)), ((), ())),
             preferred_element_type=f32,
         )
@@ -514,12 +515,8 @@
     @pl.when(step == pl.num_programs(0) - 1)
     def _():
         both = total[:comps] + total[comps:]
-        both = jnp.concatenate([both, jnp.zeros((comps, 2 * LANES - 6 * pad), f32)], axis=1)
-        summed = (
-            both
-            + pltpu.roll(both, 2 * LANES - 2 * pad, 1)
-            + pltpu.roll(both, 2 * LANES - 4 * pad, 1)
-        )[:, :LANES]
+        both = jnp.concatenate([both, jnp.zeros((comps, LANES - 4 * pad), f32)], axis=1)
+        summed = both + pltpu.roll(both, LANES - 2 * pad, 1)
         lane = lax.broadcasted_iota(jnp.int32, (comps, LANES), 1)
         summed = jnp.where(lane < 2 * pad, summed, 0.0)
         half = comps // 2
@@ -539,7 +536,7 @@
     pad = flat // rows
     assert 4 * pad <= LANES and comps % 16 == 0
     chunk = 4
-    together = 2
+    together = 4
     folded = jax.ShapeDtypeStruct((comps // 2, LANES), f32)
     inputs = ([summed] if last else []) + list(init)
     out_shape, out_specs = [folded], [pl.BlockSpec(folded.shape, lambda j: (0, 0))]
@@ -547,7 +544,7 @@
     split_spec = pl.BlockSpec((together,) + split_shape[1:], lambda j: (j, 0, 0))
     scratch = [
         pltpu.VMEM((3 * comps, 2 * LANES), bf16),
-        pltpu.VMEM((2 * comps, 6 * pad), f32),
+        pltpu.VMEM((2 * comps, 4 * pad), f32),
     ]
     params = dict(vmem_limit_bytes=24 << 20)
     if last:

time: 64.1 us -> 55.1 us (0.86)
  Pallas kernels: 61 us -> 52 us
    pallas_call x2, Pallas kernels: 32.9 us -> 23.8 us  [moments(): pl.pallas_call(functools.partial(moment_kernel, sizes, last), out_shape=o...]
where the time goes in v2:
time: 55.1 us; the launch traced here: 55 us
  Pallas kernels  52 us (94%)
  local copies, waits for them, and re-layouts  2.21 us (4%)
  between operations  0.72 us (1%)
    pallas_call x2, Pallas kernels, moments(): pl.pallas_call(functools.partial(moment_kernel, sizes, last), out_shape=o...  23.8 us
    pallas_call x1, Pallas kernels, filter_features(): pl.pallas_call(functools.partial(filter_kernel, sizes), out_shape=jax.Sha...  10.7 us
    pallas_call x1, Pallas kernels, gather_halo(): pl.pallas_call(functools.partial(halo_kernel, inlines, xlines, sizes), ou...  8.92 us
    pallas_call x1, Pallas kernels, sum_moments(): pl.pallas_call(functools.partial(sum_kernel, inlines, xlines), out_shape=...  7.74 us
    unnamed x12, local copies, waits for them, and re-layouts  2.21 us

profile of v2, /device:TPU:0, one launch (start us, length us, event | category | flops | bytes accessed | tf_op | source)
XLA Modules:
  0.0 55.0 jit_solution(7735932149012657312)
XLA Ops:
  0.6 0.0 copy-start.1
  0.6 0.0 copy-start
  0.7 0.0 copy-start.2
  0.7 0.9 %copy-done.2 = bf16[16,24,128]{2,1,0:T(8,128)(2,1)S(1)} copy-done((bf16[16,24,128]{2,1,0:T(8,128)(2,1)S(1)}, bf16[16,24,128]{2,1,0:T(8,128)(2,1)}, u32[]{:S(2)}) %copy-start.2) | copy-done | bytes 98328
  1.6 0.0 copy-start.4
  1.6 0.7 %copy-done.4 = s32[10]{0:T(128)S(1)} copy-done((s32[10]{0:T(128)S(1)}, s32[10]{0:T(128)}, u32[]{:S(2)}) %copy-start.4) | copy-done | bytes 64
  2.2 0.0 copy-start.3
  2.2 8.9 %halo.1 = (bf16[3,16,48,128]{3,2,1,0:T(8,128)(2,1)S(1)}, bf16[4,128,256]{2,1,0:T(8,128)(2,1)S(1)}, bf16[10,192,192]{2,1,0:T(8,128)(2,1)S(1)}, bf16[10,64,192]{2,1,0:T(8,128)(2,1)S(1)}) custom-call(s32[10]{0:T(128)S(1)} %copy-done.4, bf16[16,24,128]{2,1,0:T(8,128)(2,1)S(1)} %copy-done.2), custom_call_target="tpu_custom_call" | custom-call | tf_op jit(solution)/shard_map/halo/pallas_call | solution.py:217
  11.1 0.0 copy-start.5
  11.2 0.6 %copy-done.5 = s32[10]{0:T(128)S(1)} copy-done((s32[10]{0:T(128)S(1)}, s32[10]{0:T(128)}, u32[]{:S(2)}) %copy-start.5) | copy-done | bytes 64
  11.8 10.7 %filters.1.refs_0_ = f32[24,384,128]{2,1,0:T(8,128)S(1)} custom-call(s32[10]{0:T(128)S(1)} %copy-done.5, bf16[3,16,48,128]{3,2,1,0:T(8,128)(2,1)S(1)} %get-tuple-element.15.halo_ref, bf16[4,128,256]{2,1,0:T(8,128)(2,1)S(1)} %get-tuple-element.16.time_ref, bf16[10,192,192]{2,1,0:T(8,128)(2,1)S(1)} %get-tuple-element.17.x_ref, ...), custom_call_target="tpu_custom_call" | custom-call | tf_op jit(solution)/shard_map/filters/pallas_call | solution.py:321
  22.5 0.0 copy-done.1
  22.5 0.0 copy-done
  22.6 0.0 copy-done.3
  22.6 15.2 %first_pass.1 = (f32[16,128]{1,0:T(8,128)S(1)}, bf16[16,144,3072]{2,1,0:T(8,128)(2,1)S(1)}) custom-call(f32[24,384,128]{2,1,0:T(8,128)S(1)} %filters.1.refs_0_, f32[20,32]{1,0:T(8,128)S(1)} %bitcast.6, f32[20,32]{1,0:T(8,128)S(1)} %bitcast.9, f32[1,32]{1,0:T(1,128)S(1)} %bitcast.12), custom_call_target="tpu_custom_call" | custom-call | tf_op jit(solution)/shard_map/first_pass/pallas_call | solution.py:561
  37.8 8.6 %last_pass.1 = (f32[16,128]{1,0:T(8,128)S(1)}, bf16[16,32,24,128]{3,2,1,0:T(8,128)(2,1)}) custom-call(bf16[16,144,3072]{2,1,0:T(8,128)(2,1)S(1)} %get-tuple-element.19.refs_0_, f32[16,128]{1,0:T(8,128)S(1)} %get-tuple-element.20.refs_1_.refs_0_, f32[20,32]{1,0:T(8,128)S(1)} %bitcast.7, f32[20,32]{1,0:T(8,128)S(1)} %bitcast.10, f32[1,32]{1,0:T(1,128)S(1)} %bitcast.13), custom_call_target="tpu_custom_call" | custom-call | tf_op jit(solution)/shard_map/last_pass/pallas_call | solution.py:561
  46.4 7.7 %sum_moments.1.refs_1_ = f32[16,128]{1,0:T(8,128)S(1)} custom-call(f32[16,128]{1,0:T(8,128)S(1)} %get-tuple-element.22.moment_ref), custom_call_target="tpu_custom_call" | custom-call | tf_op jit(solution)/shard_map/sum_moments/pallas_call | solution.py:581
  54.1 0.8 %finish.1 = (f32[20,32]{1,0:T(8,128)}, f32[20,32]{1,0:T(8,128)}, f32[1,32]{1,0:T(1,128)}) custom-call(f32[16,128]{1,0:T(8,128)S(1)} %get-tuple-element.20.refs_1_.refs_0_, f32[16,128]{1,0:T(8,128)S(1)} %sum_moments.1.refs_1_, f32[20,32]{1,0:T(8,128)S(1)} %bitcast.8, f32[20,32]{1,0:T(8,128)S(1)} %bitcast.11, f32[1,32]{1,0:T(1,128)S(1)} %bitcast.14), custom_call_target="tpu_custom_call" | custom-call | tf_op jit(solution)/shard_map/finish/pallas_call | solution.py:615
Async XLA Ops:
  0.6 21.9 %copy-start.1 = (f32[32,20]{0,1:T(8,128)S(1)}, f32[32,20]{0,1:T(8,128)}, u32[]{:S(2)}) copy-start(f32[32,20]{0,1:T(8,128)} %param.8) | copy-start | bytes 7684
  0.6 21.9 %copy-start = (f32[32,20]{0,1:T(8,128)S(1)}, f32[32,20]{0,1:T(8,128)}, u32[]{:S(2)}) copy-start(f32[32,20]{0,1:T(8,128)} %param.7) | copy-start | bytes 7684
  0.7 0.9 %copy-start.2 = (bf16[16,24,128]{2,1,0:T(8,128)(2,1)S(1)}, bf16[16,24,128]{2,1,0:T(8,128)(2,1)}, u32[]{:S(2)}) copy-start(bf16[16,24,128]{2,1,0:T(8,128)(2,1)} %own_ref.1) | copy-start | bytes 294916
  1.6 0.7 %copy-start.4 = (s32[10]{0:T(128)S(1)}, s32[10]{0:T(128)}, u32[]{:S(2)}) copy-start(s32[10]{0:T(128)} %dir_ref.3) | copy-start | bytes 124
  2.2 20.3 %copy-start.3 = (f32[32]{0:T(128)S(1)}, f32[32]{0:T(128)}, u32[]{:S(2)}) copy-start(f32[32]{0:T(128)} %param.9) | copy-start | bytes 388
  11.1 0.7 %copy-start.5 = (s32[10]{0:T(128)S(1)}, s32[10]{0:T(128)}, u32[]{:S(2)}) copy-start(s32[10]{0:T(128)} %dir_ref.3) | copy-start | bytes 124

commit v3 on v2

--- a/solution.py
+++ b/solution.py
@@ -26,6 +26,7 @@
 bf16 = jnp.bfloat16
 VMEM = pltpu.MemorySpace.VMEM
 SMEM = pltpu.MemorySpace.SMEM
+HBM = pltpu.MemorySpace.HBM
 
 
 def round_up(value, step):
@@ -111,11 +112,19 @@
             i_ref[orient, start : start + rows, :] = value[:, : 2 * half].astype(bf16)
 
 
-def halo_kernel(inlines, xlines, sizes, dir_ref, own_ref, out_ref, time_ref, x_ref, i_ref, *sems):
-    send_sem, recv_sem, own_sem = sems
+def feature_kernel(inlines, xlines, sizes, *refs):
+    rows, cols, width, pad, orients, group = sizes
+    dir_in, own_ref, out_ref, dir_ref, halo, time_ref, x_ref, i_ref, band, cross, *sems = refs
+    send_sem, recv_sem, local_sem = sems
+    per = 8 // group
+    deep = 3 * rows
+    half = per * deep
+    span = group * width
+    pairs = cols // per
+    block = rows * width
+    steps = deep // (2 * group)
     row = lax.axis_index("inline")
     col = lax.axis_index("xline")
-    cols = sizes[1]
     mine = pl.ds(pl.multiple_of(col * cols, 8), cols)
 
     def there(side):
@@ -135,32 +144,29 @@
             device_id={"xline": lax.rem(col + shift, xlines)},
             device_id_type=MESH,
         )
-    own = pltpu.make_async_copy(own_ref, out_ref.at[1, :, mine], own_sem.at[0])
+    own = pltpu.make_async_copy(own_ref, halo.at[1, :, mine], local_sem.at[0])
     own.start()
-
-    @pl.loop(0, DIPS)
-    def _(dip):
-        time_table(dip, time_ref)
-
+    named = pltpu.make_async_copy(dir_in, dir_ref, local_sem.at[1])
+    named.start()
     sides = (row > 0).astype(jnp.int32) + (row < inlines - 1).astype(jnp.int32)
     pl.semaphore_wait(barrier, sides + xlines - 1)
 
-    def along(side):
+    def along_line(side):
         return pltpu.make_async_remote_copy(
             src_ref=own_ref,
-            dst_ref=out_ref.at[1 - side, :, mine],
+            dst_ref=halo.at[1 - side, :, mine],
             send_sem=send_sem.at[1 - side, 0],
             recv_sem=recv_sem.at[1 - side, 0],
             device_id={"inline": row + side},
             device_id_type=MESH,
         )
 
-    def across(block, shift):
+    def to_partner(part, shift):
         return pltpu.make_async_remote_copy(
-            src_ref=own_ref if block == 1 else out_ref.at[block, :, mine],
-            dst_ref=out_ref.at[block, :, mine],
-            send_sem=send_sem.at[block, shift],
-            recv_sem=recv_sem.at[block, shift],
+            src_ref=own_ref if part == 1 else halo.at[part, :, mine],
+            dst_ref=halo.at[part, :, mine],
+            send_sem=send_sem.at[part, shift],
+            recv_sem=recv_sem.at[part, shift],
             device_id={"xline": lax.rem(col + shift, xlines)},
             device_id_type=MESH,
         )
@@ -168,95 +174,32 @@
     for side in (-1, 1):
         @pl.when(there(side))
         def _(side=side):
-            along(side).start()
+            along_line(side).start()
     for shift in range(1, xlines):
-        across(1, shift).start()
+        to_partner(1, shift).start()
+
     for side in (-1, 1):
         @pl.when(jnp.logical_not(there(side)))
         def _(side=side):
-            out_ref[1 + side] = jnp.zeros(out_ref.shape[1:], out_ref.dtype)
-
-    orients = x_ref.shape[0]
-    early = orients // 2
-
-    @pl.loop(0, early)
-    def _(orient):
-        space_tables(orient, dir_ref[orient], sizes, col, x_ref, i_ref)
-
-    for side in (-1, 1):
-        @pl.when(there(side))
-        def _(side=side):
-            along(-side).wait_recv()
-            for shift in range(1, xlines):
-                across(1 + side, shift).start()
-
-    @pl.loop(early, orients)
-    def _(orient):
-        space_tables(orient, dir_ref[orient], sizes, col, x_ref, i_ref)
-
-    own.wait()
-    for shift in range(1, xlines):
-        across(1, shift).wait()
-    for side in (-1, 1):
-        @pl.when(there(side))
-        def _(side=side):
-            along(side).wait_send()
-            for shift in range(1, xlines):
-                across(1 + side, shift).wait()
-
-
-def gather_halo(traces, directions):
-    inlines, xlines = lax.axis_size("inline"), lax.axis_size("xline")
-    rows, cols, samples = traces.shape
-    orients = directions.shape[0]
-    width = xlines * cols
-    group = 4
-    assert group * width + cols <= 2 * LANES
-    per = 8 // group
-    sizes = (rows, cols, width, group)
-    return pl.pallas_call(
-        functools.partial(halo_kernel, inlines, xlines, sizes),
-        out_shape=[
-            jax.ShapeDtypeStruct((3, rows, width, samples), traces.dtype),
-            jax.ShapeDtypeStruct((DIPS, samples, 2 * samples), bf16),
-            jax.ShapeDtypeStruct((orients, 2 * cols * group, group * width), bf16),
-            jax.ShapeDtypeStruct((orients, 2 * per * rows, 2 * per * 3 * rows), bf16),
-        ],
-        in_specs=[pl.BlockSpec(memory_space=SMEM), pl.BlockSpec(memory_space=pl.ANY)],
-        out_specs=[pl.BlockSpec(memory_space=VMEM)] * 4,
-        scratch_shapes=[
-            pltpu.SemaphoreType.DMA((3, xlines)),
-            pltpu.SemaphoreType.DMA((3, xlines)),
-            pltpu.SemaphoreType.DMA((1,)),
-        ],
-        compiler_params=pltpu.CompilerParams(
-            collective_id=0, has_side_effects=True, vmem_limit_bytes=8 << 20
-        ),
-        name="halo",
-    )(directions, traces)
-
-
-def filter_kernel(sizes, dir_ref, halo_ref, time_ref, x_ref, i_ref, out_ref, band, cross):
-    rows, cols, width, pad, orients, group = sizes
-    per = 8 // group
-    deep = 3 * rows
-    half = per * deep
-    span = group * width
-    pairs = cols // per
-    block = rows * width
-
-    for y in range(cols):
-        for extra in range(pad - 2 * orients):
-            out_ref[y, pl.ds(2 * orients + extra, rows, stride=pad), :] = jnp.full(
-                (rows, LANES), 1.0 if extra == 0 else 0.0, f32
-            )
+            halo[1 + side] = jnp.zeros(halo.shape[1:], halo.dtype)
 
     @pl.loop(0, DIPS)
     def _(dip):
-        for b in range(3):
-            lines = halo_ref[b].reshape(block, LANES)
-            band[dip, b * block : (b + 1) * block, :] = jnp.dot(
-                lines, time_ref[dip], preferred_element_type=f32
+        time_table(dip, time_ref)
+
+    named.wait()
+
+    @pl.loop(0, orients)
+    def _(orient):
+        space_tables(
+            orient, dir_ref[orient], (rows, cols, width, group), col, x_ref, i_ref
+        )
+
+    def make_band(part):
+        @pl.loop(0, DIPS)
+        def _(dip):
+            band[dip, part * block : (part + 1) * block, :] = jnp.dot(
+                halo[part].reshape(block, LANES), time_ref[dip], preferred_element_type=f32
             ).astype(bf16)
 
     def across(orient, dip, step):
@@ -280,14 +223,14 @@
             for index, slot in enumerate(slots):
                 q, r = index // 2, index % 2
                 start = ((q * pairs + yp) * 2 + r) * half + step * 16
-                cross[start : start + 16, :] = jnp.concatenate(slot, axis=0).astype(bf16)
+                cross[orient, start : start + 16, :] = jnp.concatenate(slot, axis=0).astype(bf16)
 
     def along(orient, q, j):
         start = (q * pairs + 2 * j) * 2 * half
         operand = jnp.concatenate(
             [
-                cross[start : start + 2 * half, :],
-                cross[start + 2 * half : start + 4 * half, :],
+                cross[orient, start : start + 2 * half, :],
+                cross[orient, start + 2 * half : start + 4 * half, :],
             ],
             axis=1,
         )
@@ -302,34 +245,98 @@
                     (2 * j + h) * per + dy, pl.ds(2 * orient + q, rows, stride=pad), :
                 ] = size[:, h * LANES : (h + 1) * LANES]
 
-    @pl.loop(0, orients)
+    inner = range(steps // 3, 2 * steps // 3)
+    outer = [step for step in range(steps) if step not in inner]
+
+    def dip_of(orient):
+        return dir_ref[orient] // AZIMUTHS
+
+    def own_rows(first, last):
+        @pl.loop(first, last)
+        def _(orient):
+            for step in inner:
+                across(orient, dip_of(orient), step)
+
+    own.wait()
+    for shift in range(1, xlines):
+        to_partner(1, shift).wait_recv()
+    make_band(1)
+    own_rows(0, orients // 2)
+    for side in (-1, 1):
+        @pl.when(there(side))
+        def _(side=side):
+            along_line(-side).wait_recv()
+            for shift in range(1, xlines):
+                to_partner(1 + side, shift).start()
+    own_rows(orients // 2, orients)
+    for y in range(cols):
+        for extra in range(pad - 2 * orients):
+            out_ref[y, pl.ds(2 * orients + extra, rows, stride=pad), :] = jnp.full(
+                (rows, LANES), 1.0 if extra == 0 else 0.0, f32
+            )
+    for shift in range(1, xlines):
+        to_partner(1, shift).wait_send()
+    for side in (-1, 1):
+        @pl.when(there(side))
+        def _(side=side):
+            along_line(side).wait_send()
+            for shift in range(1, xlines):
+                to_partner(1 + side, shift).wait()
+    make_band(0)
+    make_band(2)
+
+    for step in outer:
+        across(0, dip_of(0), step)
+
+    pieces = [(q, j) for q in range(2) for j in range(pairs // 2)]
+    share = -(-len(pieces) // len(outer))
+
+    @pl.loop(1, orients)
     def _(orient):
-        dip = dir_ref[orient] // AZIMUTHS
-        for step in range(deep // (2 * group)):
+        dip = dip_of(orient)
+        for index, step in enumerate(outer):
             across(orient, dip, step)
-        for q in range(2):
-            for j in range(pairs // 2):
-                along(orient, q, j)
-
-
-def filter_features(halo, tables, directions, pad):
-    _, rows, width, samples = halo.shape
-    orients, height, depth = tables[1].shape
-    group = depth // width
-    cols = height // (2 * group)
+            for q, j in pieces[index * share : (index + 1) * share]:
+                along(orient - 1, q, j)
+
+    for q, j in pieces:
+        along(orients - 1, q, j)
+
+
+def make_features(traces, directions, pad):
+    inlines, xlines = lax.axis_size("inline"), lax.axis_size("xline")
+    rows, cols, samples = traces.shape
+    orients = directions.shape[0]
+    width = xlines * cols
+    group = 4
+    assert group * width + cols <= 2 * LANES
+    per = 8 // group
     sizes = (rows, cols, width, pad, orients, group)
     return pl.pallas_call(
-        functools.partial(filter_kernel, sizes),
+        functools.partial(feature_kernel, inlines, xlines, sizes),
         out_shape=jax.ShapeDtypeStruct((cols, rows * pad, samples), f32),
-        in_specs=[pl.BlockSpec(memory_space=SMEM)] + [pl.BlockSpec(memory_space=VMEM)] * 4,
+        in_specs=[pl.BlockSpec(memory_space=HBM)] * 2,
         out_specs=pl.BlockSpec(memory_space=VMEM),
         scratch_shapes=[
+            pltpu.SMEM((orients,), jnp.int32),
+            pltpu.VMEM((3, rows, width, samples), bf16),
+            pltpu.VMEM((DIPS, samples, 2 * samples), bf16),
+            pltpu.VMEM((orients, 2 * cols * group, group * width), bf16),
+            pltpu.VMEM((orients, 2 * per * rows, 2 * per * 3 * rows), bf16),
             pltpu.VMEM((DIPS, 3 * rows * width, 2 * samples), bf16),
-            pltpu.VMEM((4 * cols * 3 * rows, samples), bf16),
+            pltpu.VMEM((orients, 4 * cols * 3 * rows, samples), bf16),
+            pltpu.SemaphoreType.DMA((3, xlines)),
+            pltpu.SemaphoreType.DMA((3, xlines)),
+            pltpu.SemaphoreType.DMA((2,)),
         ],
-        compiler_params=pltpu.CompilerParams(vmem_limit_bytes=24 << 20),
-        name="filters",
-    )(directions, halo, *tables)
+        compiler_params=pltpu.CompilerParams(
+            collective_id=0, has_side_effects=True, vmem_limit_bytes=40 << 20
+        ),
+        name="features",
+    )(
+        pltpu.with_memory_space_constraint(directions, HBM),
+        pltpu.with_memory_space_constraint(traces, HBM),
+    )
 
 
 def split3(value):
@@ -634,8 +641,7 @@
     comps = init_weights.shape[0]
     cells = lax.axis_size("inline") * rows * lax.axis_size("xline") * cols * samples
     init = (init_means.T, init_variances.T, init_weights.reshape(1, comps))
-    halo, *tables = gather_halo(traces, directions)
-    features = filter_features(halo, tables, directions, pad)
+    features = make_features(traces, directions, pad)
     summed, split = moments(features, None, None, init, count, rows, cells)
     moment, posterior = moments(features, split, summed, init, count, rows, cells)
     sums = [summed, sum_moments(moment)]

time: 55.1 us -> 50.1 us (0.909)
  Pallas kernels: 52 us -> 49.2 us
  local copies, waits for them, and re-layouts: 2.21 us -> 0.01 us
    unnamed x12 -> x6, local copies, waits for them, and re-layouts: 2.21 us -> 0.01 us
    pallas_call x2 -> x1, Pallas kernels: 19.6 us -> 17.9 us  [make_features(): pl.pallas_call(functools.partial(feature_kernel, inlines, xlines, sizes),...]
    pallas_call x2, Pallas kernels: 23.8 us -> 22.7 us  [moments(): pl.pallas_call(functools.partial(moment_kernel, sizes, last), out_shape=o...]
where the time goes in v3:
time: 50.1 us; the launch traced here: 49.9 us
  Pallas kernels  49.2 us (98%)
  between operations  0.7 us (1%)
    pallas_call x2, Pallas kernels, moments(): pl.pallas_call(functools.partial(moment_kernel, sizes, last), out_shape=o...  22.7 us
    pallas_call x1, Pallas kernels, make_features(): pl.pallas_call(functools.partial(feature_kernel, inlines, xlines, sizes),...  17.9 us
    pallas_call x1, Pallas kernels, sum_moments(): pl.pallas_call(functools.partial(sum_kernel, inlines, xlines), out_shape=...  7.75 us

profile of v3, /device:TPU:0, one launch (start us, length us, event | category | flops | bytes accessed | tf_op | source)
XLA Modules:
  0.0 49.9 jit_solution(15349821573302933983)
XLA Ops:
  0.6 0.0 copy-start.2
  0.6 0.0 copy-start.1
  0.7 0.0 copy-start
  0.7 17.9 %features.1.refs_0_ = f32[24,384,128]{2,1,0:T(8,128)S(1)} custom-call(s32[10]{0:T(128)} %refs_0_.1, bf16[16,24,128]{2,1,0:T(8,128)(2,1)} %refs_1_.1), custom_call_target="tpu_custom_call" | custom-call | tf_op jit(solution)/shard_map/features/pallas_call | solution.py:315
  18.6 0.0 copy-done.2
  18.6 0.0 copy-done.1
  18.6 0.0 copy-done
  18.6 13.9 %first_pass.1 = (f32[16,128]{1,0:T(8,128)S(1)}, bf16[16,144,3072]{2,1,0:T(8,128)(2,1)S(1)}) custom-call(f32[24,384,128]{2,1,0:T(8,128)S(1)} %features.1.refs_0_, f32[20,32]{1,0:T(8,128)S(1)} %bitcast.6, f32[20,32]{1,0:T(8,128)S(1)} %bitcast.9, f32[1,32]{1,0:T(1,128)S(1)} %bitcast.12), custom_call_target="tpu_custom_call" | custom-call | tf_op jit(solution)/shard_map/first_pass/pallas_call | solution.py:568
  32.6 8.7 %last_pass.1 = (f32[16,128]{1,0:T(8,128)S(1)}, bf16[16,32,24,128]{3,2,1,0:T(8,128)(2,1)}) custom-call(bf16[16,144,3072]{2,1,0:T(8,128)(2,1)S(1)} %get-tuple-element.11.refs_0_, f32[16,128]{1,0:T(8,128)S(1)} %get-tuple-element.12.refs_1_.refs_0_, f32[20,32]{1,0:T(8,128)S(1)} %bitcast.7, f32[20,32]{1,0:T(8,128)S(1)} %bitcast.10, f32[1,32]{1,0:T(1,128)S(1)} %bitcast.13), custom_call_target="tpu_custom_call" | custom-call | tf_op jit(solution)/shard_map/last_pass/pallas_call | solution.py:568
  41.3 7.7 %sum_moments.1.refs_1_ = f32[16,128]{1,0:T(8,128)S(1)} custom-call(f32[16,128]{1,0:T(8,128)S(1)} %get-tuple-element.14.moment_ref), custom_call_target="tpu_custom_call" | custom-call | tf_op jit(solution)/shard_map/sum_moments/pallas_call | solution.py:588
  49.1 0.8 %finish.1 = (f32[20,32]{1,0:T(8,128)}, f32[20,32]{1,0:T(8,128)}, f32[1,32]{1,0:T(1,128)}) custom-call(f32[16,128]{1,0:T(8,128)S(1)} %get-tuple-element.12.refs_1_.refs_0_, f32[16,128]{1,0:T(8,128)S(1)} %sum_moments.1.refs_1_, f32[20,32]{1,0:T(8,128)S(1)} %bitcast.8, f32[20,32]{1,0:T(8,128)S(1)} %bitcast.11, f32[1,32]{1,0:T(1,128)S(1)} %bitcast.14), custom_call_target="tpu_custom_call" | custom-call | tf_op jit(solution)/shard_map/finish/pallas_call | solution.py:622
Async XLA Ops:
  0.6 18.0 %copy-start.2 = (f32[32]{0:T(128)S(1)}, f32[32]{0:T(128)}, u32[]{:S(2)}) copy-start(f32[32]{0:T(128)} %param.9) | copy-start | bytes 388
  0.6 18.0 %copy-start.1 = (f32[32,20]{0,1:T(8,128)S(1)}, f32[32,20]{0,1:T(8,128)}, u32[]{:S(2)}) copy-start(f32[32,20]{0,1:T(8,128)} %param.8) | copy-start | bytes 7684
  0.7 18.0 %copy-start = (f32[32,20]{0,1:T(8,128)S(1)}, f32[32,20]{0,1:T(8,128)}, u32[]{:S(2)}) copy-start(f32[32,20]{0,1:T(8,128)} %param.7) | copy-start | bytes 7684

commit v4 on v3

--- a/solution.py
+++ b/solution.py
@@ -382,74 +382,57 @@
     return new_means, new_spreads, jnp.broadcast_to(below / (cells + comps), (comps, LANES))
 
 
-def peer(shift, inlines, xlines):
-    me = lax.axis_index("inline") * xlines + lax.axis_index("xline")
-    other = lax.rem(me + shift, inlines * xlines)
-    return {"inline": other // xlines, "xline": lax.rem(other, xlines)}
-
-
-def greet(inlines, xlines):
-    barrier = pltpu.get_barrier_semaphore()
-    for shift in range(1, inlines * xlines):
-        pl.semaphore_signal(
-            barrier, inc=1, device_id=peer(shift, inlines, xlines), device_id_type=MESH
-        )
-
-
-def gather_sum(inlines, xlines, payload_ref, slots, send_sem, recv_sem):
-    members = inlines * xlines
-    me = lax.axis_index("inline") * xlines + lax.axis_index("xline")
-    pl.semaphore_wait(pltpu.get_barrier_semaphore(), members - 1)
-
-    def copy(shift):
+def peers(inlines, xlines):
+    row = lax.axis_index("inline")
+    col = lax.axis_index("xline")
+
+    def turned(index, shift, size):
+        moved = index + shift
+        return jnp.where(moved >= size, moved - size, moved) if shift else index
+
+    return [
+        {"inline": turned(row, down, inlines), "xline": turned(col, side, xlines)}
+        for down in range(inlines)
+        for side in range(xlines)
+        if down or side
+    ]
+
+
+def gather_sum(others, me, payload, slots, send_sem, recv_sem):
+    def copy(index):
         return pltpu.make_async_remote_copy(
-            src_ref=payload_ref,
+            src_ref=payload,
             dst_ref=slots.at[me],
-            send_sem=send_sem.at[shift],
-            recv_sem=recv_sem.at[shift],
-            device_id=peer(shift, inlines, xlines),
+            send_sem=send_sem.at[index],
+            recv_sem=recv_sem.at[index],
+            device_id=others[index],
             device_id_type=MESH,
         )
 
-    for shift in range(1, members):
-        copy(shift).start()
-    slots[me] = payload_ref[...]
-    for shift in range(1, members):
-        copy(shift).wait()
+    for index in range(len(others)):
+        copy(index).start()
+    slots[me] = payload[...]
+    for index in range(len(others)):
+        copy(index).wait()
     total = slots[0]
-    for member in range(1, members):
+    for member in range(1, len(others) + 1):
         total = total + slots[member]
     return total
 
 
-def gather_scratch(members, comps):
-    return [
-        pltpu.VMEM((members, comps // 2, LANES), f32),
-        pltpu.SemaphoreType.DMA((members,)),
-        pltpu.SemaphoreType.DMA((members,)),
-    ]
-
-
-def moment_kernel(sizes, last, *refs):
+def em_kernel(sizes, *refs):
     cols, pad, count, chunk, together, cells, inlines, xlines = sizes
-    if last:
-        split_ref, sum_ref, mean_ref, var_ref, weight_ref, *refs = refs
-        moment_ref, post_ref, table, total, wide = refs
-    else:
-        feat_ref, mean_ref, var_ref, weight_ref, *refs = refs
-        moment_ref, split_ref, table, total, shift_ref, payload, slots, send_sem, recv_sem = refs
-    step = pl.program_id(0)
+    feat_ref, mean_ref, var_ref, weight_ref, sum_ref, last_ref, post_ref, *refs = refs
+    split_ref, table, total, shift_ref, wide, payload, slots, send_sem, recv_sem = refs
     comps = mean_ref.shape[1]
-
-    @pl.when(step == 0)
-    def _():
-        if not last:
-            greet(inlines, xlines)
-        params, shift_row = first_params(mean_ref, var_ref, weight_ref)
-        if last:
-            params = next_params(sum_ref[...], params, (pad, count, cells))
-        else:
-            shift_ref[...] = column(shift_row)[:pad]
+    rows = post_ref.shape[0]
+    me = lax.axis_index("inline") * xlines + lax.axis_index("xline")
+    others = peers(inlines, xlines)
+    barrier = pltpu.get_barrier_semaphore()
+    for other in others:
+        pl.semaphore_signal(barrier, inc=1, device_id=other, device_id_type=MESH)
+
+    def prepare(params):
         lane = lax.broadcasted_iota(jnp.int32, (comps, 2 * LANES), 1)
         means = jnp.concatenate([params[0], jnp.zeros((comps, LANES), f32)], axis=1)
         spreads = jnp.concatenate([params[1], jnp.ones((comps, LANES), f32)], axis=1)
@@ -467,140 +450,139 @@
             table[index * comps : (index + 1) * comps, :] = tiled.astype(bf16)
         total[...] = jnp.zeros_like(total)
 
-    weights = table[:, : 6 * pad]
-    def scores(j, first):
-        span = slice(first * LANES, (first + chunk) * LANES)
+    def sweep(step, last):
+        weights = table[:, : 6 * pad]
+
+        def scores(j, first):
+            span = slice(first * LANES, (first + chunk) * LANES)
+            line = step * together + j
+            if last:
+                operand = split_ref[line, :, span]
+            else:
+                base = pl.multiple_of(line * pad, 8)
+                values = jnp.concatenate(
+                    [
+                        feat_ref[first + y, pl.ds(base, pad), :] - shift_ref[...]
+                        for y in range(chunk)
+                    ],
+                    axis=1,
+                )
+                both = jnp.concatenate([values, values * values], axis=0)
+                operand = jnp.concatenate(split3(both), axis=0)
+                split_ref[line, :, span] = operand
+            wide_score = jnp.dot(weights, operand, preferred_element_type=f32)
+            score = wide_score[:comps] + (
+                wide_score[comps : 2 * comps] + wide_score[2 * comps : 3 * comps]
+            )
+            return operand, score
+
+        pieces = [(j, first) for j in range(together) for first in range(0, cols, chunk)]
+        ahead = scores(*pieces[0])
+        moment = total[...]
+        for index, (j, first) in enumerate(pieces):
+            operand, score = ahead
+            if index + 1 < len(pieces):
+                ahead = scores(*pieces[index + 1])
+            exponent = jnp.exp2(score - jnp.max(score, axis=0, keepdims=True))
+            share = exponent * (1.0 / jnp.sum(exponent, axis=0, keepdims=True))
+            high = share.astype(bf16)
+            low = (share - high.astype(f32)).astype(bf16)
+            moment = moment + lax.dot_general(
+                jnp.concatenate([high, low], axis=0),
+                operand[: 4 * pad],
+                (((1,), (1,)), ((), ())),
+                preferred_element_type=f32,
+            )
+            if last:
+                for y in range(chunk):
+                    wide[pl.ds((j * comps) * cols + first + y, comps, stride=cols), :] = share[
+                        :, y * LANES : (y + 1) * LANES
+                    ]
+        total[...] = moment
         if last:
-            operand = split_ref[j, :, span]
-        else:
-            base = pl.multiple_of((step * together + j) * pad, 8)
-            values = jnp.concatenate(
-                [
-                    feat_ref[first + y, pl.ds(base, pad), :] - shift_ref[...]
-                    for y in range(chunk)
-                ],
-                axis=1,
-            )
-            both = jnp.concatenate([values, values * values], axis=0)
-            operand = jnp.concatenate(split3(both), axis=0)
-            split_ref[j, :, span] = operand
-        wide_score = jnp.dot(weights, operand, preferred_element_type=f32)
-        score = wide_score[:comps] + (
-            wide_score[comps : 2 * comps] + wide_score[2 * comps : 3 * comps]
-        )
-        return operand, score
-
-    pieces = [(j, first) for j in range(together) for first in range(0, cols, chunk)]
-    ahead = scores(*pieces[0])
-    moment = total[...]
-    for index, (j, first) in enumerate(pieces):
-        operand, score = ahead
-        if index + 1 < len(pieces):
-            ahead = scores(*pieces[index + 1])
-        exponent = jnp.exp2(score - jnp.max(score, axis=0, keepdims=True))
-        share = exponent * (1.0 / jnp.sum(exponent, axis=0, keepdims=True))
-        high = share.astype(bf16)
-        low = (share - high.astype(f32)).astype(bf16)
-        moment = moment + lax.dot_general(
-            jnp.concatenate([high, low], axis=0),
-            operand[: 4 * pad],
-            (((1,), (1,)), ((), ())),
-            preferred_element_type=f32,
-        )
-        if last:
-            for y in range(chunk):
-                wide[pl.ds((j * comps) * cols + first + y, comps, stride=cols), :] = share[
-                    :, y * LANES : (y + 1) * LANES
-                ]
-    total[...] = moment
-    if last:
-        for j in range(together):
-            for k in range(comps):
-                start = (j * comps + k) * cols
-                post_ref[j, k] = wide[start : start + cols, :].astype(bf16)
-
-    @pl.when(step == pl.num_programs(0) - 1)
-    def _():
+            for j in range(together):
+                for k in range(comps):
+                    start = (j * comps + k) * cols
+                    post_ref[step * together + j, k] = wide[start : start + cols, :].astype(bf16)
+
+    def fold():
         both = total[:comps] + total[comps:]
         both = jnp.concatenate([both, jnp.zeros((comps, LANES - 4 * pad), f32)], axis=1)
         summed = both + pltpu.roll(both, LANES - 2 * pad, 1)
         lane = lax.broadcasted_iota(jnp.int32, (comps, LANES), 1)
         summed = jnp.where(lane < 2 * pad, summed, 0.0)
         half = comps // 2
-        folded = summed[:half] + pltpu.roll(summed[half:], LANES // 2, 1)
-        if last:
-            moment_ref[...] = folded
-        else:
-            payload[...] = folded
-            moment_ref[...] = gather_sum(inlines, xlines, payload, slots, send_sem, recv_sem)
-
-
-def moments(features, split, summed, init, count, rows, cells):
-    last = summed is not None
+        return summed[:half] + pltpu.roll(summed[half:], LANES // 2, 1)
+
+    params, shift_row = first_params(mean_ref, var_ref, weight_ref)
+    shift_ref[...] = column(shift_row)[:pad]
+    prepare(params)
+    pl.loop(0, rows // together)(lambda step: sweep(step, False))
+    payload[0] = fold()
+    pl.semaphore_wait(barrier, len(others))
+    sum_ref[...] = gather_sum(
+        others, me, payload.at[0], slots.at[0], send_sem.at[0], recv_sem.at[0]
+    )
+    prepare(next_params(sum_ref[...], params, (pad, count, cells)))
+    pl.loop(0, rows // together)(lambda step: sweep(step, True))
+    payload[1] = fold()
+    last_ref[...] = gather_sum(
+        others, me, payload.at[1], slots.at[1], send_sem.at[1], recv_sem.at[1]
+    )
+
+
+def mixture(features, init, count, rows, cells):
     inlines, xlines = lax.axis_size("inline"), lax.axis_size("xline")
+    members = inlines * xlines
     comps = init[0].shape[1]
     cols, flat, samples = features.shape
     pad = flat // rows
     assert 4 * pad <= LANES and comps % 16 == 0
     chunk = 4
     together = 4
-    folded = jax.ShapeDtypeStruct((comps // 2, LANES), f32)
-    inputs = ([summed] if last else []) + list(init)
-    out_shape, out_specs = [folded], [pl.BlockSpec(folded.shape, lambda j: (0, 0))]
-    split_shape = (rows, 6 * pad, cols * samples)
-    split_spec = pl.BlockSpec((together,) + split_shape[1:], lambda j: (j, 0, 0))
-    scratch = [
-        pltpu.VMEM((3 * comps, 2 * LANES), bf16),
-        pltpu.VMEM((2 * comps, 4 * pad), f32),
-    ]
-    params = dict(vmem_limit_bytes=24 << 20)
-    if last:
-        out_shape.append(jax.ShapeDtypeStruct((rows, comps, cols, samples), bf16))
-        out_specs.append(pl.BlockSpec((together, comps, cols, samples), lambda j: (j, 0, 0, 0)))
-        scratch.append(pltpu.VMEM((together * comps * cols, samples), f32))
-    else:
-        out_shape.append(jax.ShapeDtypeStruct(split_shape, bf16))
-        out_specs.append(split_spec)
-        scratch += [pltpu.VMEM((pad, LANES), f32), pltpu.VMEM(folded.shape, f32)]
-        scratch += gather_scratch(inlines * xlines, comps)
-        params.update(collective_id=1, has_side_effects=True)
+    assert rows % together == 0 and cols % chunk == 0
+    folded = (comps // 2, LANES)
     sizes = (cols, pad, count, chunk, together, cells, inlines, xlines)
     return pl.pallas_call(
-        functools.partial(moment_kernel, sizes, last),
-        out_shape=out_shape,
-        grid=(rows // together,),
-        in_specs=[split_spec if last else pl.BlockSpec(memory_space=VMEM)]
-        + [pl.BlockSpec(array.shape, lambda j: (0, 0)) for array in inputs],
-        out_specs=out_specs,
-        scratch_shapes=scratch,
-        compiler_params=pltpu.CompilerParams(**params),
-        name="last_pass" if last else "first_pass",
-    )(split if last else features, *inputs)
-
-
-def sum_kernel(inlines, xlines, moment_ref, out_ref, slots, send_sem, recv_sem):
-    greet(inlines, xlines)
-    out_ref[...] = gather_sum(inlines, xlines, moment_ref, slots, send_sem, recv_sem)
-
-
-def sum_moments(moment):
-    inlines, xlines = lax.axis_size("inline"), lax.axis_size("xline")
-    return pl.pallas_call(
-        functools.partial(sum_kernel, inlines, xlines),
-        out_shape=jax.ShapeDtypeStruct(moment.shape, f32),
-        in_specs=[pl.BlockSpec(memory_space=VMEM)],
-        out_specs=pl.BlockSpec(memory_space=VMEM),
-        scratch_shapes=gather_scratch(inlines * xlines, 2 * moment.shape[0]),
+        functools.partial(em_kernel, sizes),
+        out_shape=[
+            jax.ShapeDtypeStruct(folded, f32),
+            jax.ShapeDtypeStruct(folded, f32),
+            jax.ShapeDtypeStruct((rows, comps, cols, samples), bf16),
+        ],
+        in_specs=[pl.BlockSpec(memory_space=VMEM)] * 4,
+        out_specs=[pl.BlockSpec(memory_space=VMEM)] * 3,
+        scratch_shapes=[
+            pltpu.VMEM((rows, 6 * pad, cols * samples), bf16),
+            pltpu.VMEM((3 * comps, 2 * LANES), bf16),
+            pltpu.VMEM((2 * comps, 4 * pad), f32),
+            pltpu.VMEM((pad, LANES), f32),
+            pltpu.VMEM((together * comps * cols, samples), f32),
+            pltpu.VMEM((2,) + folded, f32),
+            pltpu.VMEM((2, members) + folded, f32),
+            pltpu.SemaphoreType.DMA((2, members - 1)),
+            pltpu.SemaphoreType.DMA((2, members - 1)),
+        ],
         compiler_params=pltpu.CompilerParams(
-            collective_id=2, has_side_effects=True, vmem_limit_bytes=4 << 20
+            collective_id=1, has_side_effects=True, vmem_limit_bytes=36 << 20
         ),
-        name="sum_moments",
-    )(moment)
+        name="mixture",
+    )(features, *init)
 
 
 def final_kernel(sizes, *refs):
-    *sums, mean_ref, var_ref, weight_ref, mean_out, var_out, weight_out = refs
+    *sums, post_in, mean_ref, var_ref, weight_ref = refs[:-5]
+    mean_out, var_out, weight_out, post_out, sems = refs[-5:]
     count = sizes[1]
+    parts = sems.shape[0]
+    depth = post_in.shape[0] // parts
+
+    def copy(part):
+        span = pl.ds(part * depth, depth)
+        return pltpu.make_async_copy(post_in.at[span], post_out.at[span], sems.at[part])
+
+    for part in range(parts):
+        copy(part).start()
     params, shift_row = first_params(mean_ref, var_ref, weight_ref)
     for summed in sums:
         params = next_params(summed[...], params, sizes)
@@ -614,20 +596,24 @@
     mean_out[...] = turned[0][:count]
     var_out[...] = turned[1][:count]
     weight_out[...] = turned[2][:1]
-
-
-def finish(sums, init, sizes):
+    for part in range(parts):
+        copy(part).wait()
+
+
+def finish(sums, posterior, init, sizes):
     count, comps = init[0].shape
-    inputs = sums + list(init)
+    inputs = sums + [posterior] + list(init)
     return pl.pallas_call(
         functools.partial(final_kernel, sizes),
         out_shape=[
             jax.ShapeDtypeStruct((count, comps), f32),
             jax.ShapeDtypeStruct((count, comps), f32),
             jax.ShapeDtypeStruct((1, comps), f32),
+            jax.ShapeDtypeStruct(posterior.shape, posterior.dtype),
         ],
         in_specs=[pl.BlockSpec(memory_space=VMEM)] * len(inputs),
-        out_specs=[pl.BlockSpec(memory_space=VMEM)] * 3,
+        out_specs=[pl.BlockSpec(memory_space=VMEM)] * 3 + [pl.BlockSpec(memory_space=HBM)],
+        scratch_shapes=[pltpu.SemaphoreType.DMA((math.gcd(8, posterior.shape[0]),))],
         compiler_params=pltpu.CompilerParams(vmem_limit_bytes=4 << 20),
         name="finish",
     )(*inputs)
@@ -642,10 +628,8 @@
     cells = lax.axis_size("inline") * rows * lax.axis_size("xline") * cols * samples
     init = (init_means.T, init_variances.T, init_weights.reshape(1, comps))
     features = make_features(traces, directions, pad)
-    summed, split = moments(features, None, None, init, count, rows, cells)
-    moment, posterior = moments(features, split, summed, init, count, rows, cells)
-    sums = [summed, sum_moments(moment)]
-    means, spreads, weights = finish(sums, init, (pad, count, cells))
+    *sums, posterior = mixture(features, init, count, rows, cells)
+    means, spreads, weights, posterior = finish(sums, posterior, init, (pad, count, cells))
     return posterior, means.T, spreads.T, weights.reshape(comps)
 
 

time: 50.1 us -> 48.1 us (0.960)
  Pallas kernels: 49.2 us -> 47.3 us
    pallas_call x3 -> x1, Pallas kernels: 30.4 us -> 26.9 us  [mixture(): pl.pallas_call(functools.partial(em_kernel, sizes), out_shape=[jax.ShapeD...]
    pallas_call x1, Pallas kernels: 0.84 us -> 2.33 us  [finish(): pl.pallas_call(functools.partial(final_kernel, sizes), out_shape=[jax.Sha...]
where the time goes in v4:
time: 48.1 us; the launch traced here: 48 us
  Pallas kernels  47.3 us (98%)
  between operations  0.7 us (1%)
    pallas_call x1, Pallas kernels, mixture(): pl.pallas_call(functools.partial(em_kernel, sizes), out_shape=[jax.ShapeD...  26.9 us
    pallas_call x1, Pallas kernels, make_features(): pl.pallas_call(functools.partial(feature_kernel, inlines, xlines, sizes),...  18.1 us
    pallas_call x1, Pallas kernels, finish(): pl.pallas_call(functools.partial(final_kernel, sizes), out_shape=[jax.Sha...  2.33 us

profile of v4, /device:TPU:0, one launch (start us, length us, event | category | flops | bytes accessed | tf_op | source)
XLA Modules:
  0.0 48.0 jit_solution(17450721282468626644)
XLA Ops:
  0.6 0.0 copy-start.2
  0.6 0.0 copy-start.1
  0.7 0.0 copy-start
  0.7 18.1 %features.1.refs_0_ = f32[24,384,128]{2,1,0:T(8,128)S(1)} custom-call(s32[10]{0:T(128)} %refs_0_.1, bf16[16,24,128]{2,1,0:T(8,128)(2,1)} %refs_1_.1), custom_call_target="tpu_custom_call" | custom-call | tf_op jit(solution)/shard_map/features/pallas_call | solution.py:315
  18.7 0.0 copy-done.2
  18.7 0.0 copy-done.1
  18.8 0.0 copy-done
  18.8 26.9 %mixture.1 = (f32[16,128]{1,0:T(8,128)S(1)}, f32[16,128]{1,0:T(8,128)S(1)}, bf16[16,32,24,128]{3,2,1,0:T(8,128)(2,1)S(1)}) custom-call(f32[24,384,128]{2,1,0:T(8,128)S(1)} %features.1.refs_0_, f32[20,32]{1,0:T(8,128)S(1)} %bitcast.6, f32[20,32]{1,0:T(8,128)S(1)} %bitcast.8, f32[1,32]{1,0:T(1,128)S(1)} %bitcast.10), custom_call_target="tpu_custom_call" | custom-call | tf_op jit(solution)/shard_map/mixture/pallas_call | solution.py:546
  45.7 2.3 %finish.1 = (f32[20,32]{1,0:T(8,128)}, f32[20,32]{1,0:T(8,128)}, f32[1,32]{1,0:T(1,128)}, bf16[16,32,24,128]{3,2,1,0:T(8,128)(2,1)}) custom-call(f32[16,128]{1,0:T(8,128)S(1)} %get-tuple-element.11.refs_0_, f32[16,128]{1,0:T(8,128)S(1)} %get-tuple-element.12.refs_1_, bf16[16,32,24,128]{3,2,1,0:T(8,128)(2,1)S(1)} %get-tuple-element.13.refs_2_, ...), custom_call_target="tpu_custom_call" | custom-call | tf_op jit(solution)/shard_map/finish/pallas_call | solution.py:606
Async XLA Ops:
  0.6 18.1 %copy-start.2 = (f32[32]{0:T(128)S(1)}, f32[32]{0:T(128)}, u32[]{:S(2)}) copy-start(f32[32]{0:T(128)} %param.9) | copy-start | bytes 388
  0.6 18.1 %copy-start.1 = (f32[32,20]{0,1:T(8,128)S(1)}, f32[32,20]{0,1:T(8,128)}, u32[]{:S(2)}) copy-start(f32[32,20]{0,1:T(8,128)} %param.8) | copy-start | bytes 7684
  0.7 18.1 %copy-start = (f32[32,20]{0,1:T(8,128)S(1)}, f32[32,20]{0,1:T(8,128)}, u32[]{:S(2)}) copy-start(f32[32,20]{0,1:T(8,128)} %param.7) | copy-start | bytes 7684

commit v5 on v4

--- a/solution.py
+++ b/solution.py
@@ -46,9 +46,7 @@
 
 def taps(wave, difference):
     offset = (difference - HALF).astype(f32)
-    wave = jnp.concatenate([wave] * (difference.shape[1] // LANES), axis=1)
-    wave = jnp.concatenate([wave] * (difference.shape[0] // 8), axis=0)
-    phase = offset * wave
+    phase = offset * jnp.concatenate([wave] * (difference.shape[1] // LANES), axis=1)
     envelope = jnp.exp(-offset * offset / (2.0 * width_scale * width_scale)) / norm
     hit = jnp.logical_and(difference >= 0, difference < TAPS)
     real = jnp.where(hit, envelope * jnp.cos(phase), 0.0)
@@ -56,12 +54,9 @@
     return real, imag
 
 
-def angle(value, step):
-    return jnp.full((8, LANES), value.astype(f32)) * step
-
-
 def time_table(dip, time_ref):
-    wave = wavenumber * jnp.cos(angle(dip + 1, math.pi / (2 * DIPS + 2)))
+    dip_angle = jnp.full((8, LANES), (dip + 1).astype(f32)) * (math.pi / (2 * DIPS + 2))
+    wave = wavenumber * jnp.cos(dip_angle)
     sub, lane = iotas((8, LANES))
     bases = taps(wave, jnp.bitwise_and(sub - lane + HALF, LANES - 1))
     for s in range(0, LANES, 16):
@@ -74,47 +69,79 @@
         time_ref[dip, s : s + 16, :] = jnp.concatenate(pieces, axis=0).astype(bf16)
 
 
-def space_tables(orient, direction, sizes, col, x_ref, i_ref):
+def space_taps(orients, dir_ref, sizes, col, xtap_ref, itap_ref):
     rows, cols, width, group = sizes
     lanes = 2 * LANES
-    azimuth = angle(direction % AZIMUTHS, math.pi / AZIMUTHS)
-    dip_angle = angle(direction // AZIMUTHS + 1, math.pi / (2 * DIPS + 2))
+    per = 8 // group
+    height = xtap_ref.shape[1]
+    sub, lane = iotas((height, LANES))
+    azimuth, dip = jnp.zeros((height, LANES), f32), jnp.zeros((height, LANES), f32)
+    for orient in range(orients):
+        direction = dir_ref[orient]
+        here = sub == orient
+        azimuth = jnp.where(here, (direction % AZIMUTHS).astype(f32), azimuth)
+        dip = jnp.where(here, (direction // AZIMUTHS + 1).astype(f32), dip)
+    azimuth = azimuth * (math.pi / AZIMUTHS)
+    dip_angle = dip * (math.pi / (2 * DIPS + 2))
     inline_wave = wavenumber * (jnp.sin(dip_angle) * jnp.cos(azimuth))
     xline_wave = wavenumber * (jnp.sin(dip_angle) * jnp.sin(azimuth))
-
+    for index, part in enumerate(
+        taps(inline_wave, jnp.where(lane % per == 0, lane // per, -1))
+    ):
+        itap_ref[index] = part
+    lane = lax.broadcasted_iota(jnp.int32, (height, lanes), 1)
+    place = jnp.where(lane >= group * width, lane - lanes, lane)
+    for index, part in enumerate(taps(xline_wave, place - col * cols + HALF)):
+        xtap_ref[index] = part
+
+
+def space_tables(orient, sizes, xtap_ref, itap_ref, x_ref, i_ref):
+    rows, cols, width, group = sizes
+    lanes = 2 * LANES
+    per = 8 // group
     sub, lane = iotas((8, lanes))
-    row, step = sub % group, sub // group
-    place = jnp.where(lane >= group * width, lane - lanes, lane)
-    bases = taps(xline_wave, place - row * width - step - col * cols + HALF)
+    row, step = sub // per, sub % per
     mine = jnp.logical_and(lane >= row * width, lane < (row + 1) * width)
-    per = 8 // group
     for part in range(2):
+        line = jnp.broadcast_to(xtap_ref[part, pl.ds(orient, 1), :], (8, lanes))
+        both = line
+        for dy in range(1, per):
+            both = jnp.where(step == dy, roll(line, dy), both)
+        base = both
+        for r in range(1, group):
+            base = jnp.where(row == r, roll(both, r * width), base)
         for y in range(0, cols, 2 * per):
             pair = jnp.concatenate(
-                [jnp.where(mine, roll(bases[part], y + dy), 0.0) for dy in (0, per)], axis=0
+                [jnp.where(mine, roll(base, y + dy), 0.0) for dy in (0, per)], axis=0
             )
             start = (part * cols + y) * group
             x_ref[orient, start : start + 16, :] = pair[:, : group * width].astype(bf16)
 
-    deep = 3 * rows
-    half = per * deep
-    sub, lane = iotas((rows, lanes))
-    imag_in = lane >= half
-    within = jnp.where(imag_in, lane - half, lane)
-    line = (within // 8) * group + within % group
-    step = (within // group) % per
-    real, imag = taps(inline_wave, line - sub - rows + HALF)
-    blocks = [jnp.where(imag_in, -imag, real), jnp.where(imag_in, real, imag)]
+    half = per * 3 * rows
+    blank = jnp.zeros((rows, LANES), f32)
+    real, imag = [
+        pltpu.roll(
+            jnp.broadcast_to(itap_ref[part, pl.ds(orient, 1), :], (rows, LANES)),
+            per * (rows - HALF),
+            1,
+            stride=per,
+            stride_axis=0,
+        )
+        for part in range(2)
+    ]
     for dy in range(per):
-        for index, block in enumerate(blocks):
+        wide = [jnp.concatenate([roll(part, dy), blank], axis=1) for part in (real, imag)]
+        for index, value in enumerate(
+            (wide[0] - roll(wide[1], half), wide[1] + roll(wide[0], half))
+        ):
             start = (dy * 2 + index) * rows
-            value = jnp.where(step == dy, block, 0.0)
             i_ref[orient, start : start + rows, :] = value[:, : 2 * half].astype(bf16)
 
 
 def feature_kernel(inlines, xlines, sizes, *refs):
     rows, cols, width, pad, orients, group = sizes
-    dir_in, own_ref, out_ref, dir_ref, halo, time_ref, x_ref, i_ref, band, cross, *sems = refs
+    dir_in, own_ref, out_ref, dir_ref, halo, time_ref, xtap_ref, itap_ref, *refs = refs
+    x_ref, i_ref, band, cross, *sems = refs
     send_sem, recv_sem, local_sem = sems
     per = 8 // group
     deep = 3 * rows
@@ -189,18 +216,20 @@
 
     named.wait()
 
+    shape = (rows, cols, width, group)
+    space_taps(orients, dir_ref, shape, col, xtap_ref, itap_ref)
+
     @pl.loop(0, orients)
     def _(orient):
-        space_tables(
-            orient, dir_ref[orient], (rows, cols, width, group), col, x_ref, i_ref
-        )
+        space_tables(orient, shape, xtap_ref, itap_ref, x_ref, i_ref)
 
     def make_band(part):
-        @pl.loop(0, DIPS)
-        def _(dip):
-            band[dip, part * block : (part + 1) * block, :] = jnp.dot(
-                halo[part].reshape(block, LANES), time_ref[dip], preferred_element_type=f32
-            ).astype(bf16)
+        @pl.loop(0, DIPS, step=2)
+        def _(first):
+            for dip in (first, first + 1):
+                band[dip, part * block : (part + 1) * block, :] = jnp.dot(
+                    halo[part].reshape(block, LANES), time_ref[dip], preferred_element_type=f32
+                ).astype(bf16)
 
     def across(orient, dip, step):
         mixed = [
@@ -251,24 +280,27 @@
     def dip_of(orient):
         return dir_ref[orient] // AZIMUTHS
 
-    def own_rows(first, last):
-        @pl.loop(first, last)
-        def _(orient):
-            for step in inner:
-                across(orient, dip_of(orient), step)
+    def own_rows(first, last, stride):
+        @pl.loop(first, last, step=stride)
+        def _(start):
+            for orient in [start + index for index in range(stride)]:
+                for step in inner:
+                    across(orient, dip_of(orient), step)
 
     own.wait()
     for shift in range(1, xlines):
         to_partner(1, shift).wait_recv()
     make_band(1)
-    own_rows(0, orients // 2)
+    pair = 2 if orients % 2 == 0 else 1
+    early = round_up(orients // 2, pair)
+    own_rows(0, early, pair)
     for side in (-1, 1):
         @pl.when(there(side))
         def _(side=side):
             along_line(-side).wait_recv()
             for shift in range(1, xlines):
                 to_partner(1 + side, shift).start()
-    own_rows(orients // 2, orients)
+    own_rows(early, orients, pair)
     for y in range(cols):
         for extra in range(pad - 2 * orients):
             out_ref[y, pl.ds(2 * orients + extra, rows, stride=pad), :] = jnp.full(
@@ -321,6 +353,8 @@
             pltpu.SMEM((orients,), jnp.int32),
             pltpu.VMEM((3, rows, width, samples), bf16),
             pltpu.VMEM((DIPS, samples, 2 * samples), bf16),
+            pltpu.VMEM((2, round_up(orients, 8), 2 * LANES), f32),
+            pltpu.VMEM((2, round_up(orients, 8), LANES), f32),
             pltpu.VMEM((orients, 2 * cols * group, group * width), bf16),
             pltpu.VMEM((orients, 2 * per * rows, 2 * per * 3 * rows), bf16),
             pltpu.VMEM((DIPS, 3 * rows * width, 2 * samples), bf16),
@@ -366,11 +400,45 @@
     return (means - shift_row, padded(var_ref[...], 1.0)[:comps], weights), shift_row
 
 
+def packing(comps, count):
+    wide = 2 * count + 1
+    groups = LANES // wide
+    return wide, -(-comps // groups)
+
+
+def packed(summed, count, pad):
+    comps = summed.shape[0]
+    wide, height = packing(comps, count)
+    lane = lax.broadcasted_iota(jnp.int32, summed.shape, 1)
+    close = jnp.where(lane <= count, summed, pltpu.roll(summed, LANES - (pad - count - 1), 1))
+    close = jnp.where(lane < wide, close, 0.0)
+    out = close[:height]
+    for first in range(height, comps, height):
+        part = close[first : min(first + height, comps)]
+        if part.shape[0] < height:
+            blank = jnp.zeros((height - part.shape[0], LANES), f32)
+            part = jnp.concatenate([part, blank], axis=0)
+        out = out + pltpu.roll(part, (first // height) * wide, 1)
+    return out
+
+
+def unpacked(folded, comps, count, pad):
+    wide, height = packing(comps, count)
+    parts = []
+    for first in range(0, comps, height):
+        shift = (first // height) * wide
+        part = pltpu.roll(folded, LANES - shift, 1) if shift else folded
+        parts.append(part[: min(height, comps - first)])
+    close = jnp.concatenate(parts, axis=0)
+    lane = lax.broadcasted_iota(jnp.int32, close.shape, 1)
+    return jnp.where(lane <= count, close, pltpu.roll(close, pad - count - 1, 1))
+
+
 def next_params(folded, params, sizes):
     pad, count, cells = sizes
     means, spreads, _ = params
     comps = means.shape[0]
-    total = jnp.concatenate([folded, pltpu.roll(folded, LANES // 2, 1)], axis=0)
+    total = unpacked(folded, comps, count, pad)
     used = lax.broadcasted_iota(jnp.int32, (comps, LANES), 1) < count
     mass = total[:, count : count + 1]
     first = jnp.where(used, total, 0.0)
@@ -509,10 +577,7 @@
         both = total[:comps] + total[comps:]
         both = jnp.concatenate([both, jnp.zeros((comps, LANES - 4 * pad), f32)], axis=1)
         summed = both + pltpu.roll(both, LANES - 2 * pad, 1)
-        lane = lax.broadcasted_iota(jnp.int32, (comps, LANES), 1)
-        summed = jnp.where(lane < 2 * pad, summed, 0.0)
-        half = comps // 2
-        return summed[:half] + pltpu.roll(summed[half:], LANES // 2, 1)
+        return packed(summed, count, pad)
 
     params, shift_row = first_params(mean_ref, var_ref, weight_ref)
     shift_ref[...] = column(shift_row)[:pad]
@@ -541,7 +606,7 @@
     chunk = 4
     together = 4
     assert rows % together == 0 and cols % chunk == 0
-    folded = (comps // 2, LANES)
+    folded = (packing(comps, count)[1], LANES)
     sizes = (cols, pad, count, chunk, together, cells, inlines, xlines)
     return pl.pallas_call(
         functools.partial(em_kernel, sizes),

time: 48.1 us -> 46.1 us (0.958)
  Pallas kernels: 47.3 us -> 45.3 us
    pallas_call x1, Pallas kernels: 18.1 us -> 16.6 us  [make_features(): pl.pallas_call(functools.partial(feature_kernel, inlines, xlines, sizes),...]
    pallas_call x1, Pallas kernels: 26.9 us -> 26.3 us  [mixture(): pl.pallas_call(functools.partial(em_kernel, sizes), out_shape=[jax.ShapeD...]
where the time goes in v5:
time: 46.1 us; the launch traced here: 46 us
  Pallas kernels  45.3 us (98%)
  between operations  0.7 us (2%)
    pallas_call x1, Pallas kernels, mixture(): pl.pallas_call(functools.partial(em_kernel, sizes), out_shape=[jax.ShapeD...  26.3 us
    pallas_call x1, Pallas kernels, make_features(): pl.pallas_call(functools.partial(feature_kernel, inlines, xlines, sizes),...  16.6 us
    pallas_call x1, Pallas kernels, finish(): pl.pallas_call(functools.partial(final_kernel, sizes), out_shape=[jax.Sha...  2.33 us

profile of v5, /device:TPU:0, one launch (start us, length us, event | category | flops | bytes accessed | tf_op | source)
XLA Modules:
  0.0 46.0 jit_solution(3205311420247239533)
XLA Ops:
  0.6 0.0 copy-start.2
  0.6 0.0 copy-start.1
  0.7 0.0 copy-start
  0.7 16.6 %features.1.refs_0_ = f32[24,384,128]{2,1,0:T(8,128)S(1)} custom-call(s32[10]{0:T(128)} %refs_0_.1, bf16[16,24,128]{2,1,0:T(8,128)(2,1)} %refs_1_.1), custom_call_target="tpu_custom_call" | custom-call | tf_op jit(solution)/shard_map/features/pallas_call | solution.py:347
  17.3 0.0 copy-done.2
  17.3 0.0 copy-done.1
  17.3 0.0 copy-done
  17.3 26.3 %mixture.1 = (f32[11,128]{1,0:T(8,128)S(1)}, f32[11,128]{1,0:T(8,128)S(1)}, bf16[16,32,24,128]{3,2,1,0:T(8,128)(2,1)S(1)}) custom-call(f32[24,384,128]{2,1,0:T(8,128)S(1)} %features.1.refs_0_, f32[20,32]{1,0:T(8,128)S(1)} %bitcast.6, f32[20,32]{1,0:T(8,128)S(1)} %bitcast.8, f32[1,32]{1,0:T(1,128)S(1)} %bitcast.10), custom_call_target="tpu_custom_call" | custom-call | tf_op jit(solution)/shard_map/mixture/pallas_call | solution.py:611
  43.6 2.3 %finish.1 = (f32[20,32]{1,0:T(8,128)}, f32[20,32]{1,0:T(8,128)}, f32[1,32]{1,0:T(1,128)}, bf16[16,32,24,128]{3,2,1,0:T(8,128)(2,1)}) custom-call(f32[11,128]{1,0:T(8,128)S(1)} %get-tuple-element.11.refs_0_, f32[11,128]{1,0:T(8,128)S(1)} %get-tuple-element.12.refs_1_, bf16[16,32,24,128]{3,2,1,0:T(8,128)(2,1)S(1)} %get-tuple-element.13.refs_2_, ...), custom_call_target="tpu_custom_call" | custom-call | tf_op jit(solution)/shard_map/finish/pallas_call | solution.py:671
Async XLA Ops:
  0.6 16.7 %copy-start.2 = (f32[32]{0:T(128)S(1)}, f32[32]{0:T(128)}, u32[]{:S(2)}) copy-start(f32[32]{0:T(128)} %param.9) | copy-start | bytes 388
  0.6 16.7 %copy-start.1 = (f32[32,20]{0,1:T(8,128)S(1)}, f32[32,20]{0,1:T(8,128)}, u32[]{:S(2)}) copy-start(f32[32,20]{0,1:T(8,128)} %param.8) | copy-start | bytes 7684
  0.7 16.7 %copy-start = (f32[32,20]{0,1:T(8,128)S(1)}, f32[32,20]{0,1:T(8,128)}, u32[]{:S(2)}) copy-start(f32[32,20]{0,1:T(8,128)} %param.7) | copy-start | bytes 7684

commit v6 on v5

--- a/solution.py
+++ b/solution.py
@@ -323,13 +323,16 @@
     pieces = [(q, j) for q in range(2) for j in range(pairs // 2)]
     share = -(-len(pieces) // len(outer))
 
-    @pl.loop(1, orients)
-    def _(orient):
-        dip = dip_of(orient)
-        for index, step in enumerate(outer):
-            across(orient, dip, step)
-            for q, j in pieces[index * share : (index + 1) * share]:
-                along(orient - 1, q, j)
+    stride = math.gcd(orients - 1, 3)
+
+    @pl.loop(1, orients, step=stride)
+    def _(first):
+        for orient in [first + index for index in range(stride)]:
+            dip = dip_of(orient)
+            for index, step in enumerate(outer):
+                across(orient, dip, step)
+                for q, j in pieces[index * share : (index + 1) * share]:
+                    along(orient - 1, q, j)
 
     for q, j in pieces:
         along(orients - 1, q, j)
@@ -604,7 +607,7 @@
     pad = flat // rows
     assert 4 * pad <= LANES and comps % 16 == 0
     chunk = 4
-    together = 4
+    together = math.gcd(rows, 8)
     assert rows % together == 0 and cols % chunk == 0
     folded = (packing(comps, count)[1], LANES)
     sizes = (cols, pad, count, chunk, together, cells, inlines, xlines)

time: 46.1 us -> 44.8 us (0.972)
  Pallas kernels: 45.3 us -> 43.9 us
    pallas_call x1, Pallas kernels: 26.3 us -> 25.5 us  [mixture(): pl.pallas_call(functools.partial(em_kernel, sizes), out_shape=[jax.ShapeD...]
    pallas_call x1, Pallas kernels: 16.6 us -> 16 us  [make_features(): pl.pallas_call(functools.partial(feature_kernel, inlines, xlines, sizes),...]
where the time goes in v6:
time: 44.8 us; the launch traced here: 44.6 us
  Pallas kernels  43.9 us (98%)
  between operations  0.7 us (2%)
    pallas_call x1, Pallas kernels, mixture(): pl.pallas_call(functools.partial(em_kernel, sizes), out_shape=[jax.ShapeD...  25.5 us
    pallas_call x1, Pallas kernels, make_features(): pl.pallas_call(functools.partial(feature_kernel, inlines, xlines, sizes),...  16 us
    pallas_call x1, Pallas kernels, finish(): pl.pallas_call(functools.partial(final_kernel, sizes), out_shape=[jax.Sha...  2.33 us

profile of v6, /device:TPU:0, one launch (start us, length us, event | category | flops | bytes accessed | tf_op | source)
XLA Modules:
  0.0 44.6 jit_solution(7214636340626292827)
XLA Ops:
  0.6 0.0 copy-start.2
  0.6 0.0 copy-start.1
  0.7 0.0 copy-start
  0.7 16.0 %features.1.refs_0_ = f32[24,384,128]{2,1,0:T(8,128)S(1)} custom-call(s32[10]{0:T(128)} %refs_0_.1, bf16[16,24,128]{2,1,0:T(8,128)(2,1)} %refs_1_.1), custom_call_target="tpu_custom_call" | custom-call | tf_op jit(solution)/shard_map/features/pallas_call | solution.py:350
  16.7 0.0 copy-done.2
  16.7 0.0 copy-done.1
  16.7 0.0 copy-done
  16.7 25.5 %mixture.1 = (f32[11,128]{1,0:T(8,128)S(1)}, f32[11,128]{1,0:T(8,128)S(1)}, bf16[16,32,24,128]{3,2,1,0:T(8,128)(2,1)S(1)}) custom-call(f32[24,384,128]{2,1,0:T(8,128)S(1)} %features.1.refs_0_, f32[20,32]{1,0:T(8,128)S(1)} %bitcast.6, f32[20,32]{1,0:T(8,128)S(1)} %bitcast.8, f32[1,32]{1,0:T(1,128)S(1)} %bitcast.10), custom_call_target="tpu_custom_call" | custom-call | tf_op jit(solution)/shard_map/mixture/pallas_call | solution.py:614
  42.3 2.3 %finish.1 = (f32[20,32]{1,0:T(8,128)}, f32[20,32]{1,0:T(8,128)}, f32[1,32]{1,0:T(1,128)}, bf16[16,32,24,128]{3,2,1,0:T(8,128)(2,1)}) custom-call(f32[11,128]{1,0:T(8,128)S(1)} %get-tuple-element.11.refs_0_, f32[11,128]{1,0:T(8,128)S(1)} %get-tuple-element.12.refs_1_, bf16[16,32,24,128]{3,2,1,0:T(8,128)(2,1)S(1)} %get-tuple-element.13.refs_2_, ...), custom_call_target="tpu_custom_call" | custom-call | tf_op jit(solution)/shard_map/finish/pallas_call | solution.py:674
Async XLA Ops:
  0.6 16.1 %copy-start.2 = (f32[32]{0:T(128)S(1)}, f32[32]{0:T(128)}, u32[]{:S(2)}) copy-start(f32[32]{0:T(128)} %param.9) | copy-start | bytes 388
  0.6 16.1 %copy-start.1 = (f32[32,20]{0,1:T(8,128)S(1)}, f32[32,20]{0,1:T(8,128)}, u32[]{:S(2)}) copy-start(f32[32,20]{0,1:T(8,128)} %param.8) | copy-start | bytes 7684
  0.7 16.1 %copy-start = (f32[32,20]{0,1:T(8,128)S(1)}, f32[32,20]{0,1:T(8,128)}, u32[]{:S(2)}) copy-start(f32[32,20]{0,1:T(8,128)} %param.7) | copy-start | bytes 7684

commit v7 on v6

--- a/solution.py
+++ b/solution.py
@@ -224,12 +224,10 @@
         space_tables(orient, shape, xtap_ref, itap_ref, x_ref, i_ref)
 
     def make_band(part):
-        @pl.loop(0, DIPS, step=2)
-        def _(first):
-            for dip in (first, first + 1):
-                band[dip, part * block : (part + 1) * block, :] = jnp.dot(
-                    halo[part].reshape(block, LANES), time_ref[dip], preferred_element_type=f32
-                ).astype(bf16)
+        for dip in range(DIPS):
+            band[dip, part * block : (part + 1) * block, :] = jnp.dot(
+                halo[part].reshape(block, LANES), time_ref[dip], preferred_element_type=f32
+            ).astype(bf16)
 
     def across(orient, dip, step):
         mixed = [

time: 44.8 us -> 44.1 us (0.984)
  Pallas kernels: 43.9 us -> 43.3 us
    pallas_call x1, Pallas kernels: 16 us -> 15.5 us  [make_features(): pl.pallas_call(functools.partial(feature_kernel, inlines, xlines, sizes),...]
where the time goes in v7:
time: 44.1 us; the launch traced here: 44 us
  Pallas kernels  43.3 us (98%)
  between operations  0.7 us (2%)
    pallas_call x1, Pallas kernels, mixture(): pl.pallas_call(functools.partial(em_kernel, sizes), out_shape=[jax.ShapeD...  25.5 us
    pallas_call x1, Pallas kernels, make_features(): pl.pallas_call(functools.partial(feature_kernel, inlines, xlines, sizes),...  15.5 us
    pallas_call x1, Pallas kernels, finish(): pl.pallas_call(functools.partial(final_kernel, sizes), out_shape=[jax.Sha...  2.33 us

profile of v7, /device:TPU:0, one launch (start us, length us, event | category | flops | bytes accessed | tf_op | source)
XLA Modules:
  0.0 44.0 jit_solution(16834793482868241951)
XLA Ops:
  0.6 0.0 copy-start.2
  0.6 0.0 copy-start.1
  0.7 0.0 copy-start
  0.7 15.5 %features.1.refs_0_ = f32[24,384,128]{2,1,0:T(8,128)S(1)} custom-call(s32[10]{0:T(128)} %refs_0_.1, bf16[16,24,128]{2,1,0:T(8,128)(2,1)} %refs_1_.1), custom_call_target="tpu_custom_call" | custom-call | tf_op jit(solution)/shard_map/features/pallas_call | solution.py:348
  16.1 0.0 copy-done.2
  16.1 0.0 copy-done.1
  16.2 0.0 copy-done
  16.2 25.5 %mixture.1 = (f32[11,128]{1,0:T(8,128)S(1)}, f32[11,128]{1,0:T(8,128)S(1)}, bf16[16,32,24,128]{3,2,1,0:T(8,128)(2,1)S(1)}) custom-call(f32[24,384,128]{2,1,0:T(8,128)S(1)} %features.1.refs_0_, f32[20,32]{1,0:T(8,128)S(1)} %bitcast.6, f32[20,32]{1,0:T(8,128)S(1)} %bitcast.8, f32[1,32]{1,0:T(1,128)S(1)} %bitcast.10), custom_call_target="tpu_custom_call" | custom-call | tf_op jit(solution)/shard_map/mixture/pallas_call | solution.py:612
  41.7 2.3 %finish.1 = (f32[20,32]{1,0:T(8,128)}, f32[20,32]{1,0:T(8,128)}, f32[1,32]{1,0:T(1,128)}, bf16[16,32,24,128]{3,2,1,0:T(8,128)(2,1)}) custom-call(f32[11,128]{1,0:T(8,128)S(1)} %get-tuple-element.11.refs_0_, f32[11,128]{1,0:T(8,128)S(1)} %get-tuple-element.12.refs_1_, bf16[16,32,24,128]{3,2,1,0:T(8,128)(2,1)S(1)} %get-tuple-element.13.refs_2_, ...), custom_call_target="tpu_custom_call" | custom-call | tf_op jit(solution)/shard_map/finish/pallas_call | solution.py:672
Async XLA Ops:
  0.6 15.5 %copy-start.2 = (f32[32]{0:T(128)S(1)}, f32[32]{0:T(128)}, u32[]{:S(2)}) copy-start(f32[32]{0:T(128)} %param.9) | copy-start | bytes 388
  0.6 15.5 %copy-start.1 = (f32[32,20]{0,1:T(8,128)S(1)}, f32[32,20]{0,1:T(8,128)}, u32[]{:S(2)}) copy-start(f32[32,20]{0,1:T(8,128)} %param.8) | copy-start | bytes 7684
  0.7 15.5 %copy-start = (f32[32,20]{0,1:T(8,128)S(1)}, f32[32,20]{0,1:T(8,128)}, u32[]{:S(2)}) copy-start(f32[32,20]{0,1:T(8,128)} %param.7) | copy-start | bytes 7684

commit v8 on v7

--- a/solution.py
+++ b/solution.py
@@ -289,7 +289,7 @@
     for shift in range(1, xlines):
         to_partner(1, shift).wait_recv()
     make_band(1)
-    pair = 2 if orients % 2 == 0 else 1
+    pair = math.gcd(orients, 5)
     early = round_up(orients // 2, pair)
     own_rows(0, early, pair)
     for side in (-1, 1):
@@ -604,7 +604,7 @@
     cols, flat, samples = features.shape
     pad = flat // rows
     assert 4 * pad <= LANES and comps % 16 == 0
-    chunk = 4
+    chunk = 6
     together = math.gcd(rows, 8)
     assert rows % together == 0 and cols % chunk == 0
     folded = (packing(comps, count)[1], LANES)

time: 44.1 us -> 42.8 us (0.971)
  Pallas kernels: 43.3 us -> 41.9 us
    pallas_call x1, Pallas kernels: 25.5 us -> 24.6 us  [mixture(): pl.pallas_call(functools.partial(em_kernel, sizes), out_shape=[jax.ShapeD...]
    pallas_call x1, Pallas kernels: 15.5 us -> 15 us  [make_features(): pl.pallas_call(functools.partial(feature_kernel, inlines, xlines, sizes),...]
where the time goes in v8:
time: 42.8 us; the launch traced here: 42.6 us
  Pallas kernels  41.9 us (98%)
  between operations  0.7 us (2%)
    pallas_call x1, Pallas kernels, mixture(): pl.pallas_call(functools.partial(em_kernel, sizes), out_shape=[jax.ShapeD...  24.6 us
    pallas_call x1, Pallas kernels, make_features(): pl.pallas_call(functools.partial(feature_kernel, inlines, xlines, sizes),...  15 us
    pallas_call x1, Pallas kernels, finish(): pl.pallas_call(functools.partial(final_kernel, sizes), out_shape=[jax.Sha...  2.33 us

profile of v8, /device:TPU:0, one launch (start us, length us, event | category | flops | bytes accessed | tf_op | source)
XLA Modules:
  0.0 42.6 jit_solution(17678346126604422944)
XLA Ops:
  0.6 0.0 copy-start.2
  0.6 0.0 copy-start.1
  0.7 0.0 copy-start
  0.7 15.0 %features.1.refs_0_ = f32[24,384,128]{2,1,0:T(8,128)S(1)} custom-call(s32[10]{0:T(128)} %refs_0_.1, bf16[16,24,128]{2,1,0:T(8,128)(2,1)} %refs_1_.1), custom_call_target="tpu_custom_call" | custom-call | tf_op jit(solution)/shard_map/features/pallas_call | solution.py:348
  15.7 0.0 copy-done.2
  15.7 0.0 copy-done.1
  15.7 0.0 copy-done
  15.7 24.6 %mixture.1 = (f32[11,128]{1,0:T(8,128)S(1)}, f32[11,128]{1,0:T(8,128)S(1)}, bf16[16,32,24,128]{3,2,1,0:T(8,128)(2,1)S(1)}) custom-call(f32[24,384,128]{2,1,0:T(8,128)S(1)} %features.1.refs_0_, f32[20,32]{1,0:T(8,128)S(1)} %bitcast.6, f32[20,32]{1,0:T(8,128)S(1)} %bitcast.8, f32[1,32]{1,0:T(1,128)S(1)} %bitcast.10), custom_call_target="tpu_custom_call" | custom-call | tf_op jit(solution)/shard_map/mixture/pallas_call | solution.py:612
  40.3 2.3 %finish.1 = (f32[20,32]{1,0:T(8,128)}, f32[20,32]{1,0:T(8,128)}, f32[1,32]{1,0:T(1,128)}, bf16[16,32,24,128]{3,2,1,0:T(8,128)(2,1)}) custom-call(f32[11,128]{1,0:T(8,128)S(1)} %get-tuple-element.11.refs_0_, f32[11,128]{1,0:T(8,128)S(1)} %get-tuple-element.12.refs_1_, bf16[16,32,24,128]{3,2,1,0:T(8,128)(2,1)S(1)} %get-tuple-element.13.refs_2_, ...), custom_call_target="tpu_custom_call" | custom-call | tf_op jit(solution)/shard_map/finish/pallas_call | solution.py:672
Async XLA Ops:
  0.6 15.1 %copy-start.2 = (f32[32]{0:T(128)S(1)}, f32[32]{0:T(128)}, u32[]{:S(2)}) copy-start(f32[32]{0:T(128)} %param.9) | copy-start | bytes 388
  0.6 15.1 %copy-start.1 = (f32[32,20]{0,1:T(8,128)S(1)}, f32[32,20]{0,1:T(8,128)}, u32[]{:S(2)}) copy-start(f32[32,20]{0,1:T(8,128)} %param.8) | copy-start | bytes 7684
  0.7 15.1 %copy-start = (f32[32,20]{0,1:T(8,128)S(1)}, f32[32,20]{0,1:T(8,128)}, u32[]{:S(2)}) copy-start(f32[32,20]{0,1:T(8,128)} %param.7) | copy-start | bytes 7684
